TPU v7x, 32 devices: a whole 2x2x4 slice. The times are simulated.
32 devices in a mesh: expert: 4 (over z), fsdp: 8 (over y, x, core).
Axes of the slice: x: 2, y: 2, z: 4, core: 2. Of those that a mesh axis runs over, the one named last changes fastest.
Arguments:
- tokens: bfloat16 [8192, 2048], P(('expert', 'fsdp')), may hold values from -6 to 6
- cotangent: bfloat16 [8192, 2048], P(('expert', 'fsdp')), may hold values from -6 to 6
- routes: int32 [8192, 8], P(('expert', 'fsdp')), may hold values from 0 to 31, all different within a row; in each aligned block of 256 rows (0 to 255, 256 to 511, ...) at most 80 rows name the same one
- seq_lens: int32 [32, 8], P(('expert', 'fsdp')), may hold values from 1 to 128, 256 in all within a row
- attn_gain: float32 [2048], replicated, may hold values from 0.5 to 1.5
- q_gain: float32 [128], replicated, may hold values from 0.5 to 1.5
- key_norm_gain: float32 [128], replicated, may hold values from 0.5 to 1.5
- moe_gain: float32 [2048], replicated, may hold values from 0.5 to 1.5
- wq: bfloat16 [2048, 4096], P('fsdp'), may hold values from -0.125 to 0.125
- wk: bfloat16 [2048, 512], P('fsdp'), may hold values from -0.125 to 0.125
- wv: bfloat16 [2048, 512], P('fsdp'), may hold values from -0.125 to 0.125
- wo: bfloat16 [4096, 2048], P('fsdp'), may hold values from -0.5 to 0.5
- wr: bfloat16 [2048, 32], P('fsdp'), may hold values from -0.125 to 0.125
- w_gate: bfloat16 [32, 2048, 768], P(('expert', 'fsdp')), may hold values from -0.125 to 0.125
- w_up: bfloat16 [32, 2048, 768], P(('expert', 'fsdp')), may hold values from -0.125 to 0.125
- w_down: bfloat16 [32, 768, 2048], P(('expert', 'fsdp')), may hold values from -0.625 to 0.625
Outputs:
- layer_out: bfloat16 [8192, 2048], P(('expert', 'fsdp'))
- d_tokens: bfloat16 [8192, 2048], P(('expert', 'fsdp'))
- d_attn_gain: float32 [2048], replicated
- d_q_gain: float32 [128], replicated
- d_k_gain: float32 [128], replicated
- d_moe_gain: float32 [2048], replicated
- d_wq: float32 [2048, 4096], P('fsdp')
- d_wk: float32 [2048, 512], P('fsdp')
- d_wv: float32 [2048, 512], P('fsdp')
- d_wo: float32 [4096, 2048], P('fsdp')
- d_wr: float32 [2048, 32], P('fsdp')
- d_w_gate: float32 [32, 2048, 768], P(('expert', 'fsdp'))
- d_w_up: float32 [32, 2048, 768], P(('expert', 'fsdp'))
- d_w_down: float32 [32, 768, 2048], P(('expert', 'fsdp'))
Inputs may be any that keep to these rules, and one draw needn't show every extreme that they name: `routes`: each row names 8 different experts. Among the rows of one device no expert is named more than 80 times, and some device names some expert exactly 80 times. `seq_lens`: each device's 8 lengths sum to 256, and the longest is exactly 128.
All inputs are finite; a program needn't handle non-finite values.
Results may differ from a plain program's by a relative error of at most 0.02.
Values may be sent and summed in bfloat16 or wider, within the bound.
No kernel may reach another device: no remote copies, remote signals or barrier semaphores. Data moves between devices by JAX's collectives and lax.ppermute only.
A program may use at most 384 MiB of HBM per device.

v0:
```python
import jax
import jax.numpy as jnp
from jax import lax
from jax.sharding import PartitionSpec as P

QUERY_HEADS = 32
KEY_VALUE_HEADS = 4
HEAD_SIZE = 128


EPS = 1e-06
THETA = 1000000.0


def root_mean_norm(in_value, norm_gain):
    inverse = lax.rsqrt(jnp.mean(in_value * in_value, axis=-1, keepdims=True) + EPS)
    return in_value * inverse * norm_gain


def rotary_apply(in_value, rotary_angles):
    cosine = jnp.cos(rotary_angles)[:, None, :]
    sine = jnp.sin(rotary_angles)[:, None, :]
    half_size = in_value.shape[-1] // 2
    first = in_value[..., :half_size]
    second = in_value[..., half_size:]
    return jnp.concatenate(
        [first * cosine - second * sine, second * cosine + first * sine], axis=-1
    )


def layout(lengths, token_count):
    ends = jnp.cumsum(lengths)
    index = jnp.arange(token_count, dtype=jnp.int32)
    segment = jnp.sum((index[:, None] >= ends[None, :]).astype(jnp.int32), axis=1)
    starts = ends - lengths
    member = segment[:, None] == jnp.arange(lengths.shape[0], dtype=jnp.int32)[None, :]
    begins = jnp.sum(jnp.where(member, starts[None, :], 0), axis=1)
    position = (index - begins).astype(jnp.float32)
    allowed = (segment[:, None] == segment[None, :]) & (index[:, None] >= index[None, :])
    return (position, allowed)


def angles_of(position):
    exponent = jnp.arange(0, HEAD_SIZE, 2, dtype=jnp.float32) / HEAD_SIZE
    return position[:, None] * (THETA ** (-exponent))[None, :]


def heads_pre(q_proj, key_projection, q_gain, key_norm_gain, rotary_angles):
    token_count = q_proj.shape[0]
    query_rows = rotary_apply(
        root_mean_norm(q_proj.reshape(token_count, QUERY_HEADS, HEAD_SIZE), q_gain), rotary_angles
    )
    key_head_rows = rotary_apply(
        root_mean_norm(
            key_projection.reshape(token_count, KEY_VALUE_HEADS, HEAD_SIZE), key_norm_gain
        ),
        rotary_angles,
    )
    return (query_rows, key_head_rows)


def back_dot(left, right):
    return lax.dot_general(
        left, right, (((1,), (1,)), ((), ())), preferred_element_type=jnp.float32
    )


def score_of(query_rows, key_head_rows, allowed):
    token_count = query_rows.shape[0]
    grouped_heads = query_rows.reshape(
        token_count, KEY_VALUE_HEADS, QUERY_HEADS // KEY_VALUE_HEADS, HEAD_SIZE
    )
    scores = jnp.einsum(
        "qhgd,khd->hgqk", grouped_heads, key_head_rows, preferred_element_type=jnp.float32
    ) * HEAD_SIZE ** (-0.5)
    return jnp.where(allowed[None, None], scores, -1e30)


def attend(query_rows, key_head_rows, value_rows, allowed):
    token_count = query_rows.shape[0]
    scores = score_of(query_rows, key_head_rows, allowed)
    row_max = jnp.max(scores, axis=-1, keepdims=True)
    unnormed = jnp.where(allowed[None, None], jnp.exp(scores - row_max), 0.0)
    summed = jnp.sum(unnormed, axis=-1, keepdims=True)
    log_total = row_max + jnp.log(summed)
    probs = jnp.where(allowed[None, None], jnp.exp(scores - log_total), 0.0).astype(jnp.bfloat16)
    mixed = jnp.einsum("hgqk,khd->qhgd", probs, value_rows, preferred_element_type=jnp.float32)
    return (mixed.reshape(token_count, QUERY_HEADS * HEAD_SIZE).astype(jnp.bfloat16), log_total)


def attend_back(
    query_rows, key_head_rows, value_rows, head_output, head_gradient, log_total, allowed
):
    token_count = query_rows.shape[0]
    scores = score_of(query_rows, key_head_rows, allowed)
    prob_f = jnp.where(allowed[None, None], jnp.exp(scores - log_total), 0.0)
    prob_b = prob_f.astype(jnp.bfloat16)
    output_gradients = head_gradient.reshape(
        token_count, KEY_VALUE_HEADS, QUERY_HEADS // KEY_VALUE_HEADS, HEAD_SIZE
    )
    output_rows = head_output.reshape(
        token_count, KEY_VALUE_HEADS, QUERY_HEADS // KEY_VALUE_HEADS, HEAD_SIZE
    )
    value_gradient = jnp.einsum(
        "hgqk,qhgd->khd", prob_b, output_gradients, preferred_element_type=jnp.float32
    )
    d_prob = jnp.einsum(
        "qhgd,khd->hgqk", output_gradients, value_rows, preferred_element_type=jnp.float32
    )
    delta = jnp.sum(output_gradients.astype(jnp.float32) * output_rows.astype(jnp.float32), axis=-1)
    delta = jnp.transpose(delta, (1, 2, 0))[..., None]
    d_scores = (prob_f * (d_prob - delta) * HEAD_SIZE ** (-0.5)).astype(jnp.bfloat16)
    d_query = jnp.einsum(
        "hgqk,khd->qhgd", d_scores, key_head_rows, preferred_element_type=jnp.float32
    )
    grouped_heads = query_rows.reshape(
        token_count, KEY_VALUE_HEADS, QUERY_HEADS // KEY_VALUE_HEADS, HEAD_SIZE
    )
    d_key = jnp.einsum(
        "hgqk,qhgd->khd", d_scores, grouped_heads, preferred_element_type=jnp.float32
    )
    return (d_query.reshape(token_count, QUERY_HEADS, HEAD_SIZE), d_key, value_gradient)


def local_terms(x_norm, head_output, moe_in, d_q_b, d_k_b, value_block_gradient, d_attn, d_logits):
    grad_query = jnp.einsum("nd,nk->dk", x_norm, d_q_b, preferred_element_type=jnp.float32)
    grad_key = jnp.einsum("nd,nk->dk", x_norm, d_k_b, preferred_element_type=jnp.float32)
    grad_value = jnp.einsum(
        "nd,nk->dk", x_norm, value_block_gradient, preferred_element_type=jnp.float32
    )
    grad_outproj = jnp.einsum("nk,nd->kd", head_output, d_attn, preferred_element_type=jnp.float32)
    grad_router = jnp.dot(moe_in.astype(jnp.float32).T, d_logits, precision=lax.Precision.HIGHEST)
    return (grad_query, grad_key, grad_value, grad_outproj, grad_router)


def body(
    tokens,
    cotangent,
    routes,
    seq_lens,
    attn_gain,
    q_gain,
    key_norm_gain,
    moe_gain,
    wq,
    wk,
    wv,
    wo,
    wr,
    w_gate,
    w_up,
    w_down,
):
    token_count = tokens.shape[0]
    width = tokens.shape[1]
    experts = wr.shape[1]
    top_k = routes.shape[1]
    cap = max(2, token_count * top_k * 5 // (4 * experts))
    position, allowed = layout(seq_lens[0], token_count)
    rotary_angles = angles_of(position)
    x_f = tokens.astype(jnp.float32)
    x_norm_f, attn_back = jax.vjp(root_mean_norm, x_f, attn_gain)
    x_norm = x_norm_f.astype(jnp.bfloat16)
    pieces = (
        lax.all_gather(wq, "fsdp", axis=0, tiled=True),
        lax.all_gather(wk, "fsdp", axis=0, tiled=True),
        lax.all_gather(wv, "fsdp", axis=0, tiled=True),
    )
    q_proj, key_projection, value_projection = tuple(
        (jnp.dot(x_norm, piece_w, preferred_element_type=jnp.float32) for piece_w in pieces)
    )

    def pre_fn(q_in, k_in, qg_in, kg_in):
        return heads_pre(q_in, k_in, qg_in, kg_in, rotary_angles)

    (query_f, key_f), heads_back = jax.vjp(pre_fn, q_proj, key_projection, q_gain, key_norm_gain)
    query_rows = query_f.astype(jnp.bfloat16)
    key_head_rows = key_f.astype(jnp.bfloat16)
    value_rows = value_projection.reshape(token_count, KEY_VALUE_HEADS, HEAD_SIZE).astype(
        jnp.bfloat16
    )
    head_output, log_total = attend(query_rows, key_head_rows, value_rows, allowed)
    wo_all, wr_all = (
        lax.all_gather(wo, "fsdp", axis=0, tiled=True),
        lax.all_gather(wr, "fsdp", axis=0, tiled=True),
    )
    resid = x_f + jnp.dot(head_output, wo_all, preferred_element_type=jnp.float32)
    moe_norm, moe_back = jax.vjp(root_mean_norm, resid, moe_gain)
    moe_in = moe_norm.astype(jnp.bfloat16)
    logits = jnp.dot(moe_in, wr_all, preferred_element_type=jnp.float32)
    chosen = routes[:, :, None] == jnp.arange(experts, dtype=jnp.int32)[None, None, :]
    routed = jnp.sum(jnp.where(chosen, logits[:, None, :], 0.0), axis=2)
    gates = jax.nn.softmax(routed, axis=1)
    flat_routes = routes.reshape(-1)
    hits = (flat_routes[:, None] == jnp.arange(experts, dtype=jnp.int32)[None, :]).astype(jnp.int32)
    slots = jnp.sum((jnp.cumsum(hits, axis=0) - 1) * hits, axis=1)
    places = flat_routes * cap + slots
    owners = jnp.arange(flat_routes.shape[0], dtype=jnp.int32) // top_k
    outgoing = jnp.zeros((experts * cap, width), jnp.bfloat16).at[places].set(moe_in[owners])
    outgoing = outgoing.reshape(experts, cap, width)
    gate_mat = w_gate[0]
    up_mat = w_up[0]
    down_mat = w_down[0]
    hidden_width = gate_mat.shape[1]
    arrived_rows = lax.all_to_all(
        outgoing, ("expert", "fsdp"), split_axis=0, concat_axis=0, tiled=True
    )
    sources = arrived_rows.shape[0]
    slot_count = arrived_rows.shape[1]
    flat_in = arrived_rows.reshape(-1, width)
    gate_pre = jnp.dot(flat_in, gate_mat, preferred_element_type=jnp.float32)
    up_pre = jnp.dot(flat_in, up_mat, preferred_element_type=jnp.float32)
    hidden = (gate_pre * jax.nn.sigmoid(gate_pre) * up_pre).astype(jnp.bfloat16)
    result = jnp.dot(hidden, down_mat, preferred_element_type=jnp.float32).astype(jnp.bfloat16)
    result = result.reshape(sources, slot_count, width)
    returned_rows = lax.all_to_all(
        result, ("expert", "fsdp"), split_axis=0, concat_axis=0, tiled=True
    )
    gate_kept = gate_pre.reshape(sources, slot_count, hidden_width)
    up_kept = up_pre.reshape(sources, slot_count, hidden_width)
    expert_out = returned_rows.reshape(experts * cap, width)[places].reshape(
        token_count, top_k, width
    )
    out_f = expert_out.astype(jnp.float32)
    layer_out = (resid + jnp.sum(gates[:, :, None] * out_f, axis=1)).astype(jnp.bfloat16)
    d_out = cotangent.astype(jnp.float32)
    d_gates = jnp.sum(d_out[:, None, :] * out_f, axis=2)
    d_expert = (gates[:, :, None] * d_out[:, None, :]).astype(jnp.bfloat16)
    sending = (
        jnp.zeros((experts * cap, width), jnp.bfloat16).at[places].set(d_expert.reshape(-1, width))
    )
    arrived_grad = lax.all_to_all(
        sending.reshape(experts, cap, width),
        ("expert", "fsdp"),
        split_axis=0,
        concat_axis=0,
        tiled=True,
    )
    flat_grad = arrived_grad.reshape(-1, width)
    flat_in = arrived_rows.reshape(-1, width)
    gate_flat = gate_kept.reshape(-1, hidden_width)
    up_flat = up_kept.reshape(-1, hidden_width)
    sigma = jax.nn.sigmoid(gate_flat)
    active = gate_flat * sigma
    hidden = (active * up_flat).astype(jnp.bfloat16)
    d_hidden = back_dot(flat_grad, down_mat)
    d_gate_pre = (d_hidden * up_flat * sigma * (1.0 + gate_flat * (1.0 - sigma))).astype(
        jnp.bfloat16
    )
    d_up_pre = (d_hidden * active).astype(jnp.bfloat16)
    grad_down = jnp.einsum("rf,rd->fd", hidden, flat_grad, preferred_element_type=jnp.float32)
    grad_gate = jnp.einsum("rd,rf->df", flat_in, d_gate_pre, preferred_element_type=jnp.float32)
    grad_up = jnp.einsum("rd,rf->df", flat_in, d_up_pre, preferred_element_type=jnp.float32)
    back_rows = (back_dot(d_gate_pre, gate_mat) + back_dot(d_up_pre, up_mat)).astype(jnp.bfloat16)
    came_back = lax.all_to_all(
        back_rows.reshape(experts, cap, width),
        ("expert", "fsdp"),
        split_axis=0,
        concat_axis=0,
        tiled=True,
    )
    d_moe_in = jnp.sum(
        came_back.reshape(experts * cap, width)[places]
        .reshape(token_count, top_k, width)
        .astype(jnp.float32),
        axis=1,
    )
    wo_all, wr_all = (
        lax.all_gather(wo, "fsdp", axis=0, tiled=True),
        lax.all_gather(wr, "fsdp", axis=0, tiled=True),
    )
    d_routed = gates * (d_gates - jnp.sum(gates * d_gates, axis=1, keepdims=True))
    d_logits = jnp.sum(jnp.where(chosen, d_routed[:, :, None], 0.0), axis=1)
    d_moe_in = d_moe_in + jnp.dot(
        d_logits, wr_all.astype(jnp.float32).T, precision=lax.Precision.HIGHEST
    )
    d_resid_norm, d_moe_gain = moe_back(d_moe_in)
    d_resid = d_out + d_resid_norm
    d_attn = d_resid.astype(jnp.bfloat16)
    head_gradient = back_dot(d_attn, wo_all).astype(jnp.bfloat16)
    d_query, d_key, value_gradient = attend_back(
        query_rows, key_head_rows, value_rows, head_output, head_gradient, log_total, allowed
    )
    d_q_proj, d_k_proj, d_q_gain, d_k_gain = heads_back((d_query, d_key))
    d_q_b = d_q_proj.astype(jnp.bfloat16)
    d_k_b = d_k_proj.astype(jnp.bfloat16)
    value_block_gradient = value_gradient.reshape(token_count, KEY_VALUE_HEADS * HEAD_SIZE).astype(
        jnp.bfloat16
    )
    pieces = lax.all_gather((wq, wk, wv), "fsdp", axis=0, tiled=True)
    d_x_norm = (
        back_dot(d_q_b, pieces[0])
        + back_dot(d_k_b, pieces[1])
        + back_dot(value_block_gradient, pieces[2])
    )
    d_x_pre, d_attn_gain = attn_back(d_x_norm)
    d_tokens = (d_resid + d_x_pre).astype(jnp.bfloat16)
    terms = local_terms(
        x_norm, head_output, moe_in, d_q_b, d_k_b, value_block_gradient, d_attn, d_logits
    )
    summed = (
        lax.psum_scatter(
            terms[0].astype(jnp.bfloat16), "fsdp", scatter_dimension=0, tiled=True
        ).astype(jnp.float32),
        lax.psum_scatter(
            terms[1].astype(jnp.bfloat16), "fsdp", scatter_dimension=0, tiled=True
        ).astype(jnp.float32),
        lax.psum_scatter(
            terms[2].astype(jnp.bfloat16), "fsdp", scatter_dimension=0, tiled=True
        ).astype(jnp.float32),
        lax.psum_scatter(
            terms[3].astype(jnp.bfloat16), "fsdp", scatter_dimension=0, tiled=True
        ).astype(jnp.float32),
        lax.psum_scatter(
            terms[4].astype(jnp.bfloat16), "fsdp", scatter_dimension=0, tiled=True
        ).astype(jnp.float32),
    )
    shards = (
        lax.psum(summed[0].astype(jnp.bfloat16), "expert").astype(jnp.float32),
        lax.psum(summed[1].astype(jnp.bfloat16), "expert").astype(jnp.float32),
        lax.psum(summed[2].astype(jnp.bfloat16), "expert").astype(jnp.float32),
        lax.psum(summed[3].astype(jnp.bfloat16), "expert").astype(jnp.float32),
        lax.psum(summed[4].astype(jnp.bfloat16), "expert").astype(jnp.float32),
    )
    gain_sums = lax.psum((d_attn_gain, d_q_gain, d_k_gain, d_moe_gain), ("expert", "fsdp"))
    return (
        layer_out,
        d_tokens,
        gain_sums[0],
        gain_sums[1],
        gain_sums[2],
        gain_sums[3],
        shards[0],
        shards[1],
        shards[2],
        shards[3],
        shards[4],
        grad_gate[None],
        grad_up[None],
        grad_down[None],
    )


def solution(mesh):
    in_specs = (
        P(("expert", "fsdp"), None),
        P(("expert", "fsdp"), None),
        P(("expert", "fsdp"), None),
        P(("expert", "fsdp"), None),
        P(),
        P(),
        P(),
        P(),
        P("fsdp", None),
        P("fsdp", None),
        P("fsdp", None),
        P("fsdp", None),
        P("fsdp", None),
        P(("expert", "fsdp"), None, None),
        P(("expert", "fsdp"), None, None),
        P(("expert", "fsdp"), None, None),
    )
    out_specs = (
        P(("expert", "fsdp"), None),
        P(("expert", "fsdp"), None),
        P(),
        P(),
        P(),
        P(),
        P("fsdp", None),
        P("fsdp", None),
        P("fsdp", None),
        P("fsdp", None),
        P("fsdp", None),
        P(("expert", "fsdp"), None, None),
        P(("expert", "fsdp"), None, None),
        P(("expert", "fsdp"), None, None),
    )
    return jax.shard_map(body, mesh=mesh, in_specs=in_specs, out_specs=out_specs, check_vma=False)
```

profile of v0, /device:TPU:0, one launch (start us, length us, event | category | flops | bytes accessed | tf_op | source)
XLA Modules:
  0.0 1917.7 jit_solution(10859199511728378533)
XLA Ops:
  11.6 15.9 reduce-window.11
  45.7 24.6 %all-gather.7.cloned.1.call-done = bf16[2048,512]{1,0:T(8,128)(2,1)} async-done(((bf16[256,512]{1,0:T(8,128)(2,1)}), bf16[2048,512]{1,0:T(8,128)(2,1)}) %all-gather.7.cloned.1.call-update) | async-done | bytes 2097168 | tf_op jit(solution)/shard_map/all_gather | solution.py:166
  80.8 81.0 %all-gather.9.cloned.1.call-done = bf16[2048,4096]{1,0:T(8,128)(2,1)} async-done(((bf16[256,4096]{1,0:T(8,128)(2,1)}), bf16[2048,4096]{1,0:T(8,128)(2,1)}) %all-gather.9.cloned.1.call-update) | async-done | bytes 16777232 | tf_op jit(solution)/shard_map/all_gather | solution.py:165
  194.5 58.9 %all-gather.11.cloned.1.call-done = bf16[4096,2048]{1,0:T(8,128)(2,1)} async-done(((bf16[512,2048]{1,0:T(8,128)(2,1)}), bf16[4096,2048]{1,0:T(8,128)(2,1)}) %all-gather.11.cloned.1.call-update) | async-done | bytes 16777232 | tf_op jit(solution)/shard_map/all_gather | solution.py:184
  267.1 46.5 %scatter_custom_fusion = bf16[2560,2048]{1,0:T(8,128)(2,1)} fusion(s32[2048]{0:T(1024)S(1)} %bitcast.225, bf16[256,2048]{1,0:T(8,128)(2,1)} %multiply_convert_fusion.3, s32[2048]{0:T(1024)} %broadcast_clamp_fusion.1, bf16[]{:T(256)} %constant.66.clone.1), kind=kCustom, calls=%fused_computation.22 | custom fusion | bytes 10486272 | tf_op jit(solution)/shard_map/scatter | solution.py:199
  321.2 72.1 %all_gather.24 = bf16[2048,32]{0,1:T(8,128)(2,1)S(1)} all-gather(bf16[256,32]{0,1:T(8,128)(2,1)S(1)} %copy-done.74), channel_id=1, replica_groups=mesh['expert'=4,'fsdp'=8] {'fsdp'}, dimensions={0}, use_global_device_ids=true | all-gather | bytes 147456 | tf_op jit(solution)/shard_map/all_gather | solution.py:185
  397.1 19.3 %scatter_custom_fusion.1 = bf16[2560,2048]{1,0:T(8,128)(2,1)} fusion(s32[2048]{0:T(1024)S(1)} %bitcast.226, f32[256,2048]{1,0:T(8,128)} %convert_element_type.189, f32[2048]{0:T(1024)S(1)} %div.96, bf16[]{:T(256)} %constant.66.clone.1), kind=kCustom, calls=%fused_computation.16 | custom fusion | flops 8388608 | bytes 12591106 | tf_op jit(solution)/shard_map/scatter | solution.py:230
  416.4 134.0 %all-to-all-done = bf16[32,80,2048]{2,1,0:T(8,128)(2,1)} async-done(((bf16[32,80,2048]{2,1,0:T(8,128)(2,1)}), bf16[32,80,2048]{2,1,0:T(8,128)(2,1)}, u32[]{:S(2)}, u32[]{:S(2)}) %all-to-all-start) | async-done | bytes 10485792 | tf_op jit(solution)/shard_map/all_to_all | solution.py:205
  554.3 14.0 fusion.22
  581.3 205.2 %all-to-all-done.2 = bf16[32,80,2048]{2,1,0:T(8,128)(2,1)} async-done(((bf16[32,80,2048]{2,1,0:T(8,128)(2,1)}), bf16[32,80,2048]{2,1,0:T(8,128)(2,1)}, u32[]{:S(2)}, u32[]{:S(2)}) %all-to-all-start.2) | async-done | bytes 10485792 | tf_op jit(solution)/shard_map/all_to_all | solution.py:232
  786.5 19.7 %multiply_convert_fusion = (bf16[2560,768]{1,0:T(8,128)(2,1)}, bf16[2560,768]{1,0:T(8,128)(2,1)}, bf16[2560,768]{1,0:T(8,128)(2,1)}) fusion(f32[2560,768]{1,0:T(8,128)} %fusion.26, f32[2560,768]{1,0:T(8,128)} %fusion.22, bf16[2560,2048]{1,0:T(8,128)(2,1)} %bitcast.28, bf16[1,768,2048]{2,1,0:T(8,128)(2,1)S(1)} %copy-done), kind=kOutput, calls=%fused_computation.28 | convolution fusion | flops 8082554880 | bytes 41156608 | tf_op jit(solution)/shard_map/dot_general | solution.py:63
  837.2 16.6 add_convert_fusion
  853.8 202.1 %all-to-all-done.1 = bf16[32,80,2048]{2,1,0:T(8,128)(2,1)} async-done(((bf16[32,80,2048]{2,1,0:T(8,128)(2,1)}), bf16[32,80,2048]{2,1,0:T(8,128)(2,1)}, u32[]{:S(2)}, u32[]{:S(2)}) %all-to-all-start.1) | async-done | bytes 10485792 | tf_op jit(solution)/shard_map/all_to_all | solution.py:216
  1059.7 21.8 %gather_fusion = bf16[2048,2048]{1,0:T(8,128)(2,1)} fusion(bf16[2560,2048]{1,0:T(8,128)(2,1)} %bitcast.24, s32[2048]{0:T(1024)S(1)} %broadcast_clamp_fusion), kind=kCustom, calls=%fused_computation.1 | custom fusion | bytes 16785408 | tf_op jit(solution)/shard_map/gather | solution.py:221
  1091.2 200.6 %all-to-all-done.3 = bf16[32,80,2048]{2,1,0:T(8,128)(2,1)} async-done(((bf16[32,80,2048]{2,1,0:T(8,128)(2,1)}), bf16[32,80,2048]{2,1,0:T(8,128)(2,1)}, u32[]{:S(2)}, u32[]{:S(2)}) %all-to-all-start.3) | async-done | bytes 10485792 | tf_op jit(solution)/shard_map/all_to_all | solution.py:255
  1291.8 21.8 %gather_fusion.1 = bf16[2048,2048]{1,0:T(8,128)(2,1)} fusion(bf16[2560,2048]{1,0:T(8,128)(2,1)} %bitcast.30, s32[2048]{0:T(1024)S(1)} %broadcast_clamp_fusion), kind=kCustom, calls=%fused_computation.2 | custom fusion | bytes 16785408 | tf_op jit(solution)/shard_map/gather | solution.py:263
  1431.0 14.5 convolution_bitcast_fusion.1
  1446.8 14.3 convolution_bitcast_fusion.2
  1461.2 106.1 %reduce-scatter.12.cloned.1.call-done = bf16[512,2048]{1,0:T(8,128)(2,1)} async-done(((bf16[4096,2048]{1,0:T(8,128)(2,1)}), bf16[512,2048]{1,0:T(8,128)(2,1)}) %reduce-scatter.12.cloned.1.call-update) | async-done | bytes 2097168 | tf_op jit(solution)/shard_map/reduce_scatter | solution.py:311
  1567.3 119.8 %reduce-scatter.6.cloned.1.call-done = bf16[256,4096]{1,0:T(8,128)(2,1)} async-done(((bf16[2048,4096]{1,0:T(8,128)(2,1)}), bf16[256,4096]{1,0:T(8,128)(2,1)}) %reduce-scatter.6.cloned.1.call-update) | async-done | bytes 2097168 | tf_op jit(solution)/shard_map/reduce_scatter | solution.py:302
  1687.1 14.1 convolution_bitcast_fusion
  1718.2 46.4 %all-reduce.4 = (f32[2048]{0:T(1024)}, f32[128]{0:T(128)}, f32[128]{0:T(128)}, f32[2048]{0:T(1024)}) all-reduce(f32[2048]{0:T(1024)S(1)} %get-tuple-element.20, f32[128]{0:T(128)S(1)} %copy-done.83, f32[128]{0:T(128)S(1)} %copy-done.82, f32[2048]{0:T(1024)S(1)} %copy-done.64), channel_id=1, replica_groups=mesh['expert'=4,'fsdp'=8] {'expert','fsdp'}, use_global_device_ids=true, to_apply=%region_28.29 | all-reduce | flops 4352 | bytes 34816 | tf_op jit(solution)/shard_map/psum | solution.py:325
  1767.8 18.6 psum.71
  1787.0 113.1 %all-reduce.8.cloned.1.call-done = (bf16[256,4096]{1,0:T(8,128)(2,1)}, bf16[256,512]{1,0:T(8,128)(2,1)}, bf16[256,512]{1,0:T(8,128)(2,1)}, bf16[512,2048]{1,0:T(8,128)(2,1)}) async-done(((bf16[256,4096]{1,0:T(8,128)(2,1)}, bf16[256,512]{1,0:T(8,128)(2,1)}, bf16[256,512]{1,0:T(8,128)(2,1)}, bf16[512,2048]{1,0:T(8,128)(2,1)}), (bf16[256,4096]{1,0:T(8,128)(2,1)}, bf16[256,512]{1,0:T(8,128)(2,1)}, ...) | async-done | bytes 4718608 | tf_op jit(solution)/shard_map/psum | solution.py:319
  (310 shorter events, 301.2 us)
Async XLA Ops:
  7.2 779.3 %copy-start = (bf16[1,768,2048]{2,1,0:T(8,128)(2,1)S(1)}, bf16[1,768,2048]{2,1,0:T(8,128)(2,1)}, u32[]{:S(2)}) copy-start(bf16[1,768,2048]{2,1,0:T(8,128)(2,1)} %param.31) | copy-start | bytes 9437188
  7.2 33.4 %all-gather.5.cloned.1.call-start = ((), (), s32[]{:S(2)}) async-start(), calls=%async_computation.9 | async-start | bytes 2359296 | tf_op jit(solution)/shard_map/all_gather | solution.py:167
  8.0 62.3 %all-gather.7.cloned.1.call-start = ((), (), s32[]{:S(2)}) async-start(), calls=%async_computation.10 | async-start | bytes 2359296 | tf_op jit(solution)/shard_map/all_gather | solution.py:166
  8.7 153.2 %all-gather.9.cloned.1.call-start = ((), (), s32[]{:S(2)}) async-start(), calls=%async_computation.11 | async-start | bytes 18874368 | tf_op jit(solution)/shard_map/all_gather | solution.py:165
  9.4 243.9 %all-gather.11.cloned.1.call-start = ((), (), s32[]{:S(2)}) async-start(), calls=%async_computation.12 | async-start | bytes 18874368 | tf_op jit(solution)/shard_map/all_gather | solution.py:184
  32.3 41.4 %copy-start.61 = (f32[256]{0:T(256)}, f32[256]{0:T(256)S(1)}, u32[]{:S(2)}) copy-start(f32[256]{0:T(256)S(1)} %fusion.60) | copy-start | bytes 3076
  34.2 147.1 %copy-start.25 = (f32[256,64]{1,0:T(8,128)}, f32[256,64]{1,0:T(8,128)S(1)}, u32[]{:S(2)}) copy-start(f32[256,64]{1,0:T(8,128)S(1)} %get-tuple-element.47) | copy-start | bytes 196612
  34.2 147.1 %copy-start.27 = (f32[256,64]{1,0:T(8,128)}, f32[256,64]{1,0:T(8,128)S(1)}, u32[]{:S(2)}) copy-start(f32[256,64]{1,0:T(8,128)S(1)} %get-tuple-element.48) | copy-start | bytes 196612
  78.4 91.9 %copy-start.59 = (f32[256,4]{0,1:T(4,128)}, f32[256,4]{0,1:T(4,128)S(1)}, u32[]{:S(2)}) copy-start(f32[256,4]{0,1:T(4,128)S(1)} %fusion.59) | copy-start | bytes 12292
  264.6 49.1 %copy-start.77 = (f32[256]{0:T(256)}, f32[256]{0:T(256)S(1)}, u32[]{:S(2)}) copy-start(f32[256]{0:T(256)S(1)} %get-tuple-element.51) | copy-start | bytes 3076
  264.6 49.0 %copy-start.70 = (f32[256]{0:T(256)}, f32[256]{0:T(256)S(1)}, u32[]{:S(2)}) copy-start(f32[256]{0:T(256)S(1)} %fusion.61) | copy-start | bytes 3076
  313.7 236.7 %all-to-all-start = ((bf16[32,80,2048]{2,1,0:T(8,128)(2,1)}), bf16[32,80,2048]{2,1,0:T(8,128)(2,1)}, u32[]{:S(2)}, u32[]{:S(2)}) async-start(bf16[32,80,2048]{2,1,0:T(8,128)(2,1)} %bitcast.199), calls=%async_computation | async-start | bytes 20971520 | tf_op jit(solution)/shard_map/all_to_all | solution.py:205
  550.4 236.1 %all-to-all-start.2 = ((bf16[32,80,2048]{2,1,0:T(8,128)(2,1)}), bf16[32,80,2048]{2,1,0:T(8,128)(2,1)}, u32[]{:S(2)}, u32[]{:S(2)}) async-start(bf16[32,80,2048]{2,1,0:T(8,128)(2,1)} %bitcast.200), calls=%async_computation.2 | async-start | bytes 20971520 | tf_op jit(solution)/shard_map/all_to_all | solution.py:232
  819.6 236.3 %all-to-all-start.1 = ((bf16[32,80,2048]{2,1,0:T(8,128)(2,1)}), bf16[32,80,2048]{2,1,0:T(8,128)(2,1)}, u32[]{:S(2)}, u32[]{:S(2)}) async-start(bf16[32,80,2048]{2,1,0:T(8,128)(2,1)} %bitcast.209), calls=%async_computation.1 | async-start | bytes 20971520 | tf_op jit(solution)/shard_map/all_to_all | solution.py:216
  1055.9 235.9 %all-to-all-start.3 = ((bf16[32,80,2048]{2,1,0:T(8,128)(2,1)}), bf16[32,80,2048]{2,1,0:T(8,128)(2,1)}, u32[]{:S(2)}, u32[]{:S(2)}) async-start(bf16[32,80,2048]{2,1,0:T(8,128)(2,1)} %bitcast.208), calls=%async_computation.3 | async-start | bytes 20971520 | tf_op jit(solution)/shard_map/all_to_all | solution.py:255
  1059.6 401.6 %reduce-scatter.8.cloned.1.call-start = ((), (), s32[]{:S(2)}) async-start(), calls=%async_computation.14 | async-start | bytes 2359296 | tf_op jit(solution)/shard_map/reduce_scatter | solution.py:305
  1091.2 233.9 %copy-start.46 = (f32[256,32]{0,1:T(8,128)}, f32[256,32]{0,1:T(8,128)S(1)}, u32[]{:S(2)}) copy-start(f32[256,32]{0,1:T(8,128)S(1)} %select_reduce_fusion.1) | copy-start | bytes 98308
  1365.9 95.2 %reduce-scatter.10.cloned.1.call-start = ((), (), s32[]{:S(2)}) async-start(), calls=%async_computation.15 | async-start | bytes 2359296 | tf_op jit(solution)/shard_map/reduce_scatter | solution.py:308
  1375.4 191.8 %reduce-scatter.12.cloned.1.call-start = ((), (), s32[]{:S(2)}) async-start(), calls=%async_computation.16 | async-start | bytes 18874368 | tf_op jit(solution)/shard_map/reduce_scatter | solution.py:311
  1385.9 301.1 %reduce-scatter.6.cloned.1.call-start = ((), (), s32[]{:S(2)}) async-start(), calls=%async_computation.13 | async-start | bytes 18874368 | tf_op jit(solution)/shard_map/reduce_scatter | solution.py:302
  1430.9 336.8 %reduce-scatter.14.cloned.1.call-start = ((), (), s32[]{:S(2)}) async-start(), calls=%async_computation.17 | async-start | bytes 147456 | tf_op jit(solution)/shard_map/reduce_scatter | solution.py:314
  1446.8 453.3 %all-reduce.8.cloned.1.call-start = ((), (), s32[]{:S(2)}) async-start(), calls=%async_computation.18 | async-start | bytes 9437184 | tf_op jit(solution)/shard_map/psum | solution.py:319
  1715.7 48.9 %copy-start.76 = (f32[256]{0:T(256)S(1)}, f32[256]{0:T(256)}, u32[]{:S(2)}) copy-start(f32[256]{0:T(256)} %copy-done.75) | copy-start | bytes 3076
  1715.7 48.9 %copy-start.11 = (f32[256,2048]{1,0:T(8,128)S(1)}, f32[256,2048]{1,0:T(8,128)}, u32[]{:S(2)}) copy-start(f32[256,2048]{1,0:T(8,128)} %get-tuple-element.41) | copy-start | bytes 6291460
  (77 other events, 483.6 us)
Sparse Core Ops, SparseCore 0:
  9.9 30.6 all-gather.4
  42.5 27.7 all-gather.6
  72.1 89.7 all-gather.8
  163.6 89.7 all-gather.10
  1366.1 37.0 reduce-scatter.7
  1406.3 41.1 reduce-scatter.9
  1451.0 116.1 reduce-scatter.11
  1570.8 116.1 reduce-scatter.5
  1690.6 33.5 reduce-scatter.13
  1726.7 173.3 all-reduce.7
where the time goes:
time: 1930 us; the launch traced here: 1920 us
  waiting for transfers between devices  1250 us (65%)
  matrix products  244 us (13%)
  blocking collectives  137 us (7%)
  local copies, waits for them, and re-layouts  128 us (7%)
  other arithmetic  122 us (6%)
    all_to_all x1, waiting for transfers between devices, body(): lax.all_to_all(sending.reshape(experts, cap, width), ('expert', 'fsdp'),...  205 us
    all_to_all x1, waiting for transfers between devices, body(): lax.all_to_all(result, ('expert', 'fsdp'), split_axis=0, concat_axis=0, t...  202 us
    all_to_all x1, waiting for transfers between devices, body(): lax.all_to_all(back_rows.reshape(experts, cap, width), ('expert', 'fsdp')...  201 us
    all_to_all x1, waiting for transfers between devices, body(): lax.all_to_all(outgoing, ('expert', 'fsdp'), split_axis=0, concat_axis=0,...  134 us
    reduce_scatter x1, waiting for transfers between devices, body(): lax.psum_scatter(terms[0].astype(jnp.bfloat16), 'fsdp', scatter_dimension...  120 us
    psum x1, waiting for transfers between devices, body(): lax.psum(summed[0].astype(jnp.bfloat16), 'expert').astype(jnp.float32)  113 us
    reduce_scatter x1, waiting for transfers between devices, body(): lax.psum_scatter(terms[3].astype(jnp.bfloat16), 'fsdp', scatter_dimension...  106 us
    all_gather x1, waiting for transfers between devices, body(): lax.all_gather(wq, 'fsdp', axis=0, tiled=True)  81 us
  transfers between devices with their start and end apart: 14, of which 11 were waited for; matrix products, arithmetic and copies ran while one was open for 16% of the time, Pallas kernels for 0%

commit v1 on v0

v1 whole, which is shorter than its diff:
```python
import jax
import jax.numpy as jnp
from jax import lax
from jax.sharding import PartitionSpec as P

QUERY_HEADS = 32
KEY_VALUE_HEADS = 4
HEAD_SIZE = 128


EPS = 1e-06
THETA = 1000000.0


def root_mean_norm(in_value, norm_gain):
    inverse = lax.rsqrt(jnp.mean(in_value * in_value, axis=-1, keepdims=True) + EPS)
    return in_value * inverse * norm_gain


def rotary_apply(in_value, rotary_angles):
    cosine = jnp.cos(rotary_angles)[:, None, :]
    sine = jnp.sin(rotary_angles)[:, None, :]
    half_size = in_value.shape[-1] // 2
    first = in_value[..., :half_size]
    second = in_value[..., half_size:]
    return jnp.concatenate(
        [first * cosine - second * sine, second * cosine + first * sine], axis=-1
    )


def layout(lengths, token_count):
    ends = jnp.cumsum(lengths)
    index = jnp.arange(token_count, dtype=jnp.int32)
    segment = jnp.sum((index[:, None] >= ends[None, :]).astype(jnp.int32), axis=1)
    starts = ends - lengths
    member = segment[:, None] == jnp.arange(lengths.shape[0], dtype=jnp.int32)[None, :]
    begins = jnp.sum(jnp.where(member, starts[None, :], 0), axis=1)
    position = (index - begins).astype(jnp.float32)
    allowed = (segment[:, None] == segment[None, :]) & (index[:, None] >= index[None, :])
    return (position, allowed)


def angles_of(position):
    exponent = jnp.arange(0, HEAD_SIZE, 2, dtype=jnp.float32) / HEAD_SIZE
    return position[:, None] * (THETA ** (-exponent))[None, :]


def heads_pre(q_proj, key_projection, q_gain, key_norm_gain, rotary_angles):
    token_count = q_proj.shape[0]
    query_rows = rotary_apply(
        root_mean_norm(q_proj.reshape(token_count, QUERY_HEADS, HEAD_SIZE), q_gain), rotary_angles
    )
    key_head_rows = rotary_apply(
        root_mean_norm(
            key_projection.reshape(token_count, KEY_VALUE_HEADS, HEAD_SIZE), key_norm_gain
        ),
        rotary_angles,
    )
    return (query_rows, key_head_rows)


def back_dot(left, right):
    return lax.dot_general(
        left, right, (((1,), (1,)), ((), ())), preferred_element_type=jnp.float32
    )


def score_of(query_rows, key_head_rows, allowed):
    token_count = query_rows.shape[0]
    grouped_heads = query_rows.reshape(
        token_count, KEY_VALUE_HEADS, QUERY_HEADS // KEY_VALUE_HEADS, HEAD_SIZE
    )
    scores = jnp.einsum(
        "qhgd,khd->hgqk", grouped_heads, key_head_rows, preferred_element_type=jnp.float32
    ) * HEAD_SIZE ** (-0.5)
    return jnp.where(allowed[None, None], scores, -1e30)


def attend(query_rows, key_head_rows, value_rows, allowed):
    token_count = query_rows.shape[0]
    scores = score_of(query_rows, key_head_rows, allowed)
    row_max = jnp.max(scores, axis=-1, keepdims=True)
    unnormed = jnp.where(allowed[None, None], jnp.exp(scores - row_max), 0.0)
    summed = jnp.sum(unnormed, axis=-1, keepdims=True)
    log_total = row_max + jnp.log(summed)
    probs = jnp.where(allowed[None, None], jnp.exp(scores - log_total), 0.0).astype(jnp.bfloat16)
    mixed = jnp.einsum("hgqk,khd->qhgd", probs, value_rows, preferred_element_type=jnp.float32)
    return (mixed.reshape(token_count, QUERY_HEADS * HEAD_SIZE).astype(jnp.bfloat16), log_total)


def attend_back(
    query_rows, key_head_rows, value_rows, head_output, head_gradient, log_total, allowed
):
    token_count = query_rows.shape[0]
    scores = score_of(query_rows, key_head_rows, allowed)
    prob_f = jnp.where(allowed[None, None], jnp.exp(scores - log_total), 0.0)
    prob_b = prob_f.astype(jnp.bfloat16)
    output_gradients = head_gradient.reshape(
        token_count, KEY_VALUE_HEADS, QUERY_HEADS // KEY_VALUE_HEADS, HEAD_SIZE
    )
    output_rows = head_output.reshape(
        token_count, KEY_VALUE_HEADS, QUERY_HEADS // KEY_VALUE_HEADS, HEAD_SIZE
    )
    value_gradient = jnp.einsum(
        "hgqk,qhgd->khd", prob_b, output_gradients, preferred_element_type=jnp.float32
    )
    d_prob = jnp.einsum(
        "qhgd,khd->hgqk", output_gradients, value_rows, preferred_element_type=jnp.float32
    )
    delta = jnp.sum(output_gradients.astype(jnp.float32) * output_rows.astype(jnp.float32), axis=-1)
    delta = jnp.transpose(delta, (1, 2, 0))[..., None]
    d_scores = (prob_f * (d_prob - delta) * HEAD_SIZE ** (-0.5)).astype(jnp.bfloat16)
    d_query = jnp.einsum(
        "hgqk,khd->qhgd", d_scores, key_head_rows, preferred_element_type=jnp.float32
    )
    grouped_heads = query_rows.reshape(
        token_count, KEY_VALUE_HEADS, QUERY_HEADS // KEY_VALUE_HEADS, HEAD_SIZE
    )
    d_key = jnp.einsum(
        "hgqk,qhgd->khd", d_scores, grouped_heads, preferred_element_type=jnp.float32
    )
    return (d_query.reshape(token_count, QUERY_HEADS, HEAD_SIZE), d_key, value_gradient)


def route_places(ids, wanted):
    hit = jnp.any(ids[..., :, None, :] == wanted[:, None], axis=-3)
    tokens = ids.shape[-1]
    before = jnp.triu(jnp.ones((tokens, tokens), jnp.bfloat16), 1)
    slots = jnp.dot(hit.astype(jnp.bfloat16), before, preferred_element_type=jnp.float32)
    return jnp.where(hit, slots, -1.0)


def dot32(left, right):
    return jnp.dot(left, right, preferred_element_type=jnp.float32)


def first_dot(left, right):
    return lax.dot_general(
        left, right, (((0,), (0,)), ((), ())), preferred_element_type=jnp.float32
    )


def body(
    tokens,
    cotangent,
    routes,
    seq_lens,
    attn_gain,
    q_gain,
    key_norm_gain,
    moe_gain,
    wq,
    wk,
    wv,
    wo,
    wr,
    w_gate,
    w_up,
    w_down,
):
    token_count, width = tokens.shape
    experts = wr.shape[1]
    top_k = routes.shape[1]
    n_exp = lax.axis_size("expert")
    n_fsdp = lax.axis_size("fsdp")
    everyone = ("expert", "fsdp")
    cap = max(2, token_count * top_k * 5 // (4 * experts))
    plane = lax.axis_index("expert")
    column = lax.axis_index("fsdp")
    rel = range(n_exp)
    bf = jnp.bfloat16

    def across(value, r):
        return lax.ppermute(value, "expert", [(i, i ^ r) for i in range(n_exp)]) if r else value

    def in_plane(value):
        return lax.all_to_all(value, "fsdp", split_axis=0, concat_axis=0, tiled=True)

    routes_t = routes.T
    routes_all = lax.all_gather(routes_t, everyone, axis=0, tiled=True)
    routes_all = routes_all.reshape(n_exp, n_fsdp, top_k, token_count)
    planes_rel = jnp.arange(n_exp, dtype=jnp.int32) ^ plane
    routes_rel = jnp.take(routes_all, planes_rel, axis=0)
    routes_col = lax.dynamic_index_in_dim(routes_rel, column, 1, keepdims=False)
    plane_experts = plane * n_fsdp + jnp.arange(n_fsdp, dtype=jnp.int32)
    slot_ids = jnp.arange(cap, dtype=jnp.int32).astype(jnp.float32)
    col_places = route_places(routes_col, plane_experts)
    picks = (col_places[:, :, None, :] == slot_ids[:, None]).astype(bf)
    picks = picks.reshape(n_exp, n_fsdp * cap, token_count)
    own_expert = plane * n_fsdp + column
    expert_places = route_places(routes_rel, own_expert[None])[:, :, 0, :]
    own_places = route_places(routes_t, jnp.arange(experts, dtype=jnp.int32))

    def dispatch(value):
        out = []
        for r in rel:
            rows = dot32(picks[r], across(value, r)).astype(bf)
            out.append(in_plane(rows.reshape(n_fsdp, cap, width)).reshape(n_fsdp * cap, width))
        return out

    def combine(parts):
        total = None
        for r in rel:
            back = in_plane(parts[r].reshape(n_fsdp, cap, width)).reshape(n_fsdp * cap, width)
            summed = first_dot(picks[r], back)
            if r:
                summed = across(summed.astype(bf), r).astype(jnp.float32)
            total = summed if total is None else total + summed
        return total

    grad_rows = dispatch(cotangent)

    position, allowed = layout(seq_lens[0], token_count)
    rotary_angles = angles_of(position)
    x_f = tokens.astype(jnp.float32)
    x_norm_f, attn_back = jax.vjp(root_mean_norm, x_f, attn_gain)
    x_norm = x_norm_f.astype(bf)
    q_cols = wq.shape[1]
    k_cols = wk.shape[1]
    pad = -experts % 128
    packed = jnp.concatenate([wq, wk, wv, jnp.pad(wr, ((0, 0), (0, pad)))], axis=1)
    w_in = lax.all_gather(packed, "fsdp", axis=0, tiled=True)
    wr_all = w_in[:, q_cols + 2 * k_cols : q_cols + 2 * k_cols + experts]
    wo_all = lax.all_gather(wo, "fsdp", axis=0, tiled=True)
    proj = dot32(x_norm, w_in)
    q_proj = proj[:, :q_cols]
    key_projection = proj[:, q_cols : q_cols + k_cols]
    value_projection = proj[:, q_cols + k_cols : q_cols + 2 * k_cols]

    def pre_fn(q_in, k_in, qg_in, kg_in):
        return heads_pre(q_in, k_in, qg_in, kg_in, rotary_angles)

    (query_f, key_f), heads_back = jax.vjp(pre_fn, q_proj, key_projection, q_gain, key_norm_gain)
    query_rows = query_f.astype(bf)
    key_head_rows = key_f.astype(bf)
    value_rows = value_projection.reshape(token_count, KEY_VALUE_HEADS, HEAD_SIZE).astype(bf)
    head_output, log_total = attend(query_rows, key_head_rows, value_rows, allowed)
    resid = x_f + dot32(head_output, wo_all)
    moe_norm, moe_back = jax.vjp(root_mean_norm, resid, moe_gain)
    moe_in = moe_norm.astype(bf)

    flat_in = dispatch(moe_in)
    logits = lax.dot_general(
        wr_all, moe_in, (((0,), (1,)), ((), ())), preferred_element_type=jnp.float32
    )
    chosen = own_places >= 0.0
    top_logit = jnp.max(jnp.where(chosen, logits, -jnp.inf), axis=0, keepdims=True)
    raised = jnp.where(chosen, jnp.exp(jnp.where(chosen, logits - top_logit, 0.0)), 0.0)
    gates = raised / jnp.sum(raised, axis=0, keepdims=True)
    gates_all = lax.all_gather(gates, everyone, axis=0, tiled=True)
    gates_all = gates_all.reshape(n_exp, n_fsdp, experts, token_count)
    gate_own = lax.dynamic_index_in_dim(gates_all, own_expert, 2, keepdims=False)
    gate_own = jnp.take(gate_own, planes_rel, axis=0)
    slot_gates = jnp.sum(
        jnp.where(expert_places[:, :, None, :] == slot_ids[:, None], gate_own[:, :, None, :], 0.0),
        axis=3,
    )
    gate_mat = w_gate[0]
    up_mat = w_up[0]
    down_mat = w_down[0]
    back_parts, out_parts, hid_parts, dg_parts, du_parts, gate_grads = [], [], [], [], [], []
    for r in rel:
        gate_pre = dot32(flat_in[r], gate_mat)
        up_pre = dot32(flat_in[r], up_mat)
        d_plain = back_dot(grad_rows[r], down_mat)
        scale = slot_gates[r].reshape(-1, 1)
        sigma = jax.nn.sigmoid(gate_pre)
        active = gate_pre * sigma
        hidden = active * up_pre
        gate_grads.append(
            jnp.sum(hidden.astype(bf).astype(jnp.float32) * d_plain, axis=1).reshape(n_fsdp, cap)
        )
        d_hidden = d_plain * scale
        d_gate_pre = (d_hidden * up_pre * sigma * (1.0 + gate_pre * (1.0 - sigma))).astype(bf)
        d_up_pre = (d_hidden * active).astype(bf)
        hidden_scaled = (hidden * scale).astype(bf)
        back_parts.append((back_dot(d_gate_pre, gate_mat) + back_dot(d_up_pre, up_mat)).astype(bf))
        out_parts.append(dot32(hidden_scaled, down_mat).astype(bf))
        hid_parts.append(hidden_scaled)
        dg_parts.append(d_gate_pre)
        du_parts.append(d_up_pre)
    d_moe_in = combine(back_parts)
    gate_grads = jnp.take(jnp.stack(gate_grads), planes_rel, axis=0)
    gate_grads = lax.all_gather(gate_grads.reshape(n_exp * n_fsdp, cap), everyone, axis=0, tiled=True)
    gate_grads = gate_grads.reshape(experts, n_exp * n_fsdp, cap)
    gate_grads = lax.dynamic_index_in_dim(gate_grads, own_expert, 1, keepdims=False)
    d_gates = jnp.sum(
        jnp.where(own_places[:, None, :] == slot_ids[:, None], gate_grads[:, :, None], 0.0), axis=1
    )
    d_logits = gates * (d_gates - jnp.sum(gates * d_gates, axis=0, keepdims=True))
    d_moe_in = d_moe_in + lax.dot_general(
        d_logits,
        wr_all.astype(jnp.float32),
        (((0,), (1,)), ((), ())),
        precision=lax.Precision.HIGHEST,
        preferred_element_type=jnp.float32,
    )
    d_out = cotangent.astype(jnp.float32)
    d_resid_norm, d_moe_gain = moe_back(d_moe_in)
    d_resid = d_out + d_resid_norm
    d_attn = d_resid.astype(bf)

    d_attn_all = lax.all_gather(d_attn, "fsdp", axis=0, tiled=True)
    d_logits_all = lax.all_gather(d_logits, "fsdp", axis=0, tiled=True)
    x_norm_all = lax.all_gather(x_norm, "fsdp", axis=0, tiled=True)
    heads_cols = lax.all_to_all(head_output, "fsdp", split_axis=1, concat_axis=0, tiled=True)
    moe_cols = lax.all_to_all(moe_in, "fsdp", split_axis=1, concat_axis=0, tiled=True)
    head_gradient = back_dot(d_attn, wo_all).astype(bf)
    d_query, d_key, value_gradient = attend_back(
        query_rows, key_head_rows, value_rows, head_output, head_gradient, log_total, allowed
    )
    d_q_proj, d_k_proj, d_q_gain, d_k_gain = heads_back((d_query, d_key))
    d_q_b = d_q_proj.astype(bf)
    d_k_b = d_k_proj.astype(bf)
    d_v_b = value_gradient.reshape(token_count, k_cols).astype(bf)
    d_proj = jnp.concatenate(
        [d_q_b, d_k_b, d_v_b, jnp.zeros((token_count, experts + pad), bf)], axis=1
    )
    d_x_norm = back_dot(d_proj, w_in)
    d_x_pre, d_attn_gain = attn_back(d_x_norm)
    d_tokens = (d_resid + d_x_pre).astype(bf)

    grad_outproj = first_dot(heads_cols, d_attn_all)
    q_part = q_cols // n_fsdp
    k_part = k_cols // n_fsdp
    d_cols = jnp.concatenate(
        [
            d_q_b.reshape(token_count, n_fsdp, q_part),
            d_k_b.reshape(token_count, n_fsdp, k_part),
            d_v_b.reshape(token_count, n_fsdp, k_part),
        ],
        axis=2,
    ).reshape(token_count, -1)
    d_cols = lax.all_to_all(d_cols, "fsdp", split_axis=1, concat_axis=0, tiled=True)
    grad_in = first_dot(x_norm_all, d_cols).astype(bf)
    grad_in = lax.all_to_all(grad_in, "fsdp", split_axis=0, concat_axis=1, tiled=True)
    d_logits_all = d_logits_all.reshape(n_fsdp, experts, token_count)
    d_logits_all = jnp.transpose(d_logits_all, (1, 0, 2)).reshape(experts, n_fsdp * token_count)
    grad_router = lax.dot_general(
        moe_cols.astype(jnp.float32),
        d_logits_all,
        (((0,), (1,)), ((), ())),
        precision=lax.Precision.HIGHEST,
        preferred_element_type=jnp.float32,
    )
    grad_outproj = lax.psum(grad_outproj.astype(bf), "expert").astype(jnp.float32)
    grad_router = jnp.pad(grad_router.astype(bf), ((0, 0), (0, pad)))
    grad_rows_in = jnp.concatenate([grad_in, grad_router], axis=1)
    grad_rows_in = lax.psum(grad_rows_in, "expert").astype(jnp.float32)
    in_cols = n_fsdp * (q_part + 2 * k_part)
    split = grad_rows_in[:, :in_cols].reshape(-1, n_fsdp, q_part + 2 * k_part)
    grad_query = split[:, :, :q_part].reshape(-1, q_cols)
    grad_key = split[:, :, q_part : q_part + k_part].reshape(-1, k_cols)
    grad_value = split[:, :, q_part + k_part :].reshape(-1, k_cols)
    grad_router = grad_rows_in[:, in_cols : in_cols + experts]

    rows_in = jnp.concatenate(flat_in, axis=0)
    grad_gate = first_dot(rows_in, jnp.concatenate(dg_parts, axis=0))
    grad_up = first_dot(rows_in, jnp.concatenate(du_parts, axis=0))
    grad_down = first_dot(jnp.concatenate(hid_parts, axis=0), jnp.concatenate(grad_rows, axis=0))
    layer_out = (resid + combine(out_parts)).astype(bf)
    gain_sums = lax.psum((d_attn_gain, d_q_gain, d_k_gain, d_moe_gain), everyone)
    return (
        layer_out,
        d_tokens,
        gain_sums[0],
        gain_sums[1],
        gain_sums[2],
        gain_sums[3],
        grad_query,
        grad_key,
        grad_value,
        grad_outproj,
        grad_router,
        grad_gate[None],
        grad_up[None],
        grad_down[None],
    )


def solution(mesh):
    in_specs = (
        P(("expert", "fsdp"), None),
        P(("expert", "fsdp"), None),
        P(("expert", "fsdp"), None),
        P(("expert", "fsdp"), None),
        P(),
        P(),
        P(),
        P(),
        P("fsdp", None),
        P("fsdp", None),
        P("fsdp", None),
        P("fsdp", None),
        P("fsdp", None),
        P(("expert", "fsdp"), None, None),
        P(("expert", "fsdp"), None, None),
        P(("expert", "fsdp"), None, None),
    )
    out_specs = (
        P(("expert", "fsdp"), None),
        P(("expert", "fsdp"), None),
        P(),
        P(),
        P(),
        P(),
        P("fsdp", None),
        P("fsdp", None),
        P("fsdp", None),
        P("fsdp", None),
        P("fsdp", None),
        P(("expert", "fsdp"), None, None),
        P(("expert", "fsdp"), None, None),
        P(("expert", "fsdp"), None, None),
    )
    return jax.shard_map(body, mesh=mesh, in_specs=in_specs, out_specs=out_specs, check_vma=False)
```

time: 1930 us -> 1460 us (0.76)
  waiting for transfers between devices: 1250 us -> 490 us
  blocking collectives: 137 us -> 301 us
  starting transfers between devices: 16.8 us -> 157 us
  matrix products: 244 us -> 318 us
  other arithmetic: 122 us -> 80.3 us
  local copies, waits for them, and re-layouts: 128 us -> 88.5 us
    all_to_all x4 -> x20, waiting for transfers between devices: 742 us -> 231 us  [the longest x16 192 us: in_plane(): lax.all_to_all(value, 'fsdp', split_axis=0, concat_axis=0, tiled=True)]
    reduce_scatter x5 -> x0, waiting for transfers between devices: 226 us -> none  [the longest x1 120 us: body(): lax.psum_scatter(terms[0].astype(jnp.bfloat16), 'fsdp', scatter_dimension...]
    ppermute x0 -> x12, waiting for transfers between devices: none -> 163 us  [across(): lax.ppermute(value, 'expert', [(i, i ^ r) for i in range(n_exp)])]
    all_gather x4 -> x5, waiting for transfers between devices: 170 us -> 54.4 us  [the longest x1 42.6 us: body(): gates_all = lax.all_gather(gates, everyone, axis=0, tiled=True)]
    psum x2 -> x1, blocking collectives: 65 us -> 163 us  [body(): lax.psum((d_attn_gain, d_q_gain, d_k_gain, d_moe_gain), everyone)]
    all_to_all x4 -> x20, starting transfers between devices: 16.4 us -> 100 us  [the longest x16 82.1 us: in_plane(): lax.all_to_all(value, 'fsdp', split_axis=0, concat_axis=0, tiled=True)]
    dot_general x17 -> x41, matrix products: 142 us -> 217 us  [the longest x22 110 us: dot32(): return jnp.dot(left, right, preferred_element_type=jnp.float32)]
    psum x1, waiting for transfers between devices: 113 us -> 40.7 us  [body(): grad_rows_in = lax.psum(grad_rows_in, 'expert').astype(jnp.float32)]
  transfers between devices with their start and end apart: 14 -> 38, of which waited for: 11 -> 21; matrix products, arithmetic and copies ran while one was open for 16% -> 30% of each run, Pallas kernels for 0% -> 0%
where the time goes in v1:
time: 1460 us; the launch traced here: 1450 us
  waiting for transfers between devices  490 us (34%)
  matrix products  318 us (22%)
  blocking collectives  301 us (21%)
  starting transfers between devices  157 us (11%)
  local copies, waits for them, and re-layouts  88.5 us (6%)
  other arithmetic  80.3 us (6%)
  between operations  16 us (1%)
    all_to_all x16, waiting for transfers between devices, in_plane(): lax.all_to_all(value, 'fsdp', split_axis=0, concat_axis=0, tiled=True)  192 us
    psum x1, blocking collectives, body(): lax.psum((d_attn_gain, d_q_gain, d_k_gain, d_moe_gain), everyone)  163 us
    ppermute x12, waiting for transfers between devices, across(): lax.ppermute(value, 'expert', [(i, i ^ r) for i in range(n_exp)])  163 us
    dot_general x22, matrix products, dot32(): return jnp.dot(left, right, preferred_element_type=jnp.float32)  110 us
    dot_general x13, matrix products, first_dot(): lax.dot_general(left, right, (((0,), (0,)), ((), ())), preferred_element_...  96.2 us
    all_to_all x16, starting transfers between devices, in_plane(): lax.all_to_all(value, 'fsdp', split_axis=0, concat_axis=0, tiled=True)  82.1 us
    all_gather x1, blocking collectives, body(): routes_all = lax.all_gather(routes_t, everyone, axis=0, tiled=True)  81.3 us
    dot_general x14, matrix products, back_dot(): lax.dot_general(left, right, (((1,), (1,)), ((), ())), preferred_element_...  77 us
  transfers between devices with their start and end apart: 38, of which 21 were waited for; matrix products, arithmetic and copies ran while one was open for 30% of the time, Pallas kernels for 0%

profile of v1, /device:TPU:0, one launch (start us, length us, event | category | flops | bytes accessed | tf_op | source)
XLA Modules:
  0.0 1451.1 jit_solution(18311995456401937074)
XLA Ops:
  17.7 81.3 %all_gather.26 = s32[256,256]{1,0:T(8,128)} all-gather(s32[8,256]{1,0:T(8,128)S(1)} %bitcast.379), channel_id=1, replica_groups=mesh['expert'=4,'fsdp'=8] {'expert','fsdp'}, dimensions={0}, use_global_device_ids=true | all-gather | bytes 270336 | tf_op jit(solution)/shard_map/all_gather | solution.py:180
  188.0 13.8 all-to-all-start.10
  214.8 47.8 %all-to-all-done.10 = bf16[8,80,2048]{2,1,0:T(8,128)(2,1)} async-done(((bf16[8,80,2048]{2,1,0:T(8,128)(2,1)}), bf16[8,80,2048]{2,1,0:T(8,128)(2,1)}, u32[]{:S(2)}, u32[]{:S(2)}) %all-to-all-start.10) | async-done | bytes 2621472 | tf_op jit(solution)/shard_map/all_to_all | solution.py:177
  311.2 23.8 %collective-permute-done = bf16[256,2048]{1,0:T(8,128)(2,1)S(1)} collective-permute-done((bf16[256,2048]{1,0:T(8,128)(2,1)}, bf16[256,2048]{1,0:T(8,128)(2,1)S(1)}, u32[]{:S(2)}, u32[]{:S(2)}) %collective-permute-start) | collective-permute-done | bytes 1048608 | tf_op jit(solution)/shard_map/ppermute | solution.py:174
  352.8 20.4 %collective-permute-done.10 = bf16[256,2048]{1,0:T(8,128)(2,1)} collective-permute-done((bf16[256,2048]{1,0:T(8,128)(2,1)}, bf16[256,2048]{1,0:T(8,128)(2,1)}, u32[]{:S(2)}, u32[]{:S(2)}) %collective-permute-start.10) | collective-permute-done | bytes 1048608 | tf_op jit(solution)/shard_map/ppermute | solution.py:174
  379.5 83.4 %collective-permute-done.2 = bf16[256,2048]{1,0:T(8,128)(2,1)} collective-permute-done((bf16[256,2048]{1,0:T(8,128)(2,1)}, bf16[256,2048]{1,0:T(8,128)(2,1)}, u32[]{:S(2)}, u32[]{:S(2)}) %collective-permute-start.2) | collective-permute-done | bytes 1048608 | tf_op jit(solution)/shard_map/ppermute | solution.py:174
  489.6 13.5 all-to-all-done.4
  584.9 41.0 %all_gather.28 = f32[1024,80]{1,0:T(8,128)S(1)} all-gather(f32[32,80]{1,0:T(8,128)S(1)} %bitcast_select_fusion.1), channel_id=1, replica_groups=mesh['expert'=4,'fsdp'=8] {'expert','fsdp'}, dimensions={0}, use_global_device_ids=true | all-gather | bytes 337920 | tf_op jit(solution)/shard_map/all_gather | solution.py:284
  637.9 42.6 %all-gather.10.cloned.1.call-done = f32[1024,256]{1,0:T(8,128)} async-done(((f32[32,256]{1,0:T(8,128)}), f32[1024,256]{1,0:T(8,128)}) %all-gather.10.cloned.1.call-update) | async-done | bytes 1048592 | tf_op jit(solution)/shard_map/all_gather | solution.py:250
  712.2 33.8 %all-to-all-done.11 = bf16[8,80,2048]{2,1,0:T(8,128)(2,1)} async-done(((bf16[8,80,2048]{2,1,0:T(8,128)(2,1)}), bf16[8,80,2048]{2,1,0:T(8,128)(2,1)}, u32[]{:S(2)}, u32[]{:S(2)}) %all-to-all-start.11) | async-done | bytes 2621472 | tf_op jit(solution)/shard_map/all_to_all | solution.py:177
  762.3 21.4 %all-to-all-done.13 = bf16[8,80,2048]{2,1,0:T(8,128)(2,1)} async-done(((bf16[8,80,2048]{2,1,0:T(8,128)(2,1)}), bf16[8,80,2048]{2,1,0:T(8,128)(2,1)}, u32[]{:S(2)}, u32[]{:S(2)}) %all-to-all-start.13) | async-done | bytes 2621472 | tf_op jit(solution)/shard_map/all_to_all | solution.py:177
  799.5 20.9 %all-to-all-done.15 = bf16[8,80,2048]{2,1,0:T(8,128)(2,1)} async-done(((bf16[8,80,2048]{2,1,0:T(8,128)(2,1)}), bf16[8,80,2048]{2,1,0:T(8,128)(2,1)}, u32[]{:S(2)}, u32[]{:S(2)}) %all-to-all-start.15) | async-done | bytes 2621472 | tf_op jit(solution)/shard_map/all_to_all | solution.py:177
  845.1 15.5 %all_gather.30 = f32[256,256]{1,0:T(8,128)S(1)} all-gather(f32[32,256]{1,0:T(8,128)S(1)} %subtract_multiply_fusion), channel_id=1, replica_groups=mesh['expert'=4,'fsdp'=8] {'fsdp'}, dimensions={0}, use_global_device_ids=true | all-gather | bytes 294912 | tf_op jit(solution)/shard_map/all_gather | solution.py:304
  872.9 32.8 %collective-permute-done.9 = bf16[256,2048]{1,0:T(8,128)(2,1)} collective-permute-done((bf16[256,2048]{1,0:T(8,128)(2,1)}, bf16[256,2048]{1,0:T(8,128)(2,1)}, u32[]{:S(2)}, u32[]{:S(2)}) %collective-permute-start.9) | collective-permute-done | bytes 1048608 | tf_op jit(solution)/shard_map/ppermute | solution.py:174
  977.4 14.0 fusion.39
  991.4 24.9 %all-to-all-done.16 = bf16[256,8,640]{0,2,1:T(8,128)(2,1)} async-done(((bf16[256,8,640]{0,2,1:T(8,128)(2,1)}), bf16[256,8,640]{0,2,1:T(8,128)(2,1)}, u32[]{:S(2)}, u32[]{:S(2)}) %all-to-all-start.16) | async-done | bytes 2621472 | tf_op jit(solution)/shard_map/all_to_all | solution.py:334
  1041.0 14.2 all-to-all-done.3
  1064.9 13.7 fusion.42
  1078.5 13.5 all-to-all-done.17
  1096.5 14.0 fusion.45
  1152.2 27.5 %collective-permute-start.1 = (bf16[256,2048]{1,0:T(8,128)(2,1)}, bf16[256,2048]{1,0:T(8,128)(2,1)}, u32[]{:S(2)}, u32[]{:S(2)}) collective-permute-start(bf16[256,2048]{1,0:T(8,128)(2,1)} %convolution_convert_fusion.20), channel_id=1, source_target_pairs={{0,8},{8,0},{16,24},{24,16},{1,9},{9,1},{17,25},{25,17},{2,10},{10... | collective-permute-start | bytes 3145736 | tf_op jit(solution)/shard_map/ppermute | solution.py:174
  1194.5 16.6 %fusion.102 = (f32[2048]{0:T(1024)S(1)}, f32[256]{0:T(256)S(1)}, f32[256,2048]{1,0:T(8,128)}) fusion(bf16[256,2048]{1,0:T(8,128)(2,1)} %param.16, f32[256]{0:T(256)S(1)} %copy-done.90, f32[2048]{0:T(1024)S(1)} %copy-done.73, bf16[2048,5248]{1,0:T(8,128)(2,1)} %all-gather.6.cloned.1.call-done, bf16[256,512]{0,1:T(8,128)(2,1)} %bitcast.373, ...), kind=kOutput, calls=%fused_computation.147 | convolution fusion | flops 5517342720 | bytes 27291904 | tf_op jit(solution)/shard_map/dot_general | solution.py:63
  1211.1 163.2 %all-reduce.6 = (f32[2048]{0:T(1024)}, f32[128]{0:T(128)}, f32[128]{0:T(128)}, f32[2048]{0:T(1024)}) all-reduce(f32[2048]{0:T(1024)S(1)} %get-tuple-element.102, f32[128]{0:T(128)S(1)} %copy-done.100, f32[128]{0:T(128)S(1)} %copy-done.99, f32[2048]{0:T(1024)S(1)} %copy-done.78), channel_id=1, replica_groups=mesh['expert'=4,'fsdp'=8] {'expert','fsdp'}, use_global_device_ids=true, to_apply=%region_27.28 | all-reduce | flops 4352 | bytes 34816 | tf_op jit(solution)/shard_map/psum | solution.py:362
  1382.5 40.7 %all-reduce.10.cloned.1.call-done = (bf16[256,5248]{0,1:T(8,128)(2,1)}, bf16[512,2048]{1,0:T(8,128)(2,1)}) async-done(((bf16[256,5248]{0,1:T(8,128)(2,1)}, bf16[512,2048]{1,0:T(8,128)(2,1)}), (bf16[256,5248]{0,1:T(8,128)(2,1)}, bf16[512,2048]{1,0:T(8,128)(2,1)})) %all-reduce.10.cloned.1.call-update) | async-done | bytes 4784144 | tf_op jit(solution)/shard_map/psum | solution.py:349
  (468 shorter events, 600.8 us)
Async XLA Ops:
  7.2 129.2 %all-gather.6.cloned.1.call-start = ((), (), s32[]{:S(2)}) async-start(), calls=%async_computation.20 | async-start | bytes 24182784 | tf_op jit(solution)/shard_map/all_gather | solution.py:222
  11.2 260.5 %all-gather.8.cloned.1.call-start = ((), (), s32[]{:S(2)}) async-start(), calls=%async_computation.21 | async-start | bytes 18874368 | tf_op jit(solution)/shard_map/all_gather | solution.py:224
  12.0 109.9 %collective-permute-start.6 = (bf16[256,2048]{1,0:T(8,128)(2,1)}, bf16[256,2048]{1,0:T(8,128)(2,1)}, u32[]{:S(2)}, u32[]{:S(2)}) collective-permute-start(bf16[256,2048]{1,0:T(8,128)(2,1)} %param.17), channel_id=1, source_target_pairs={{0,8},{8,0},{16,24},{24,16},{1,9},{9,1},{17,25},{25,17},{2,10},{10... | collective-permute-start | bytes 3145736 | tf_op jit(solution)/shard_map/ppermute | solution.py:174
  15.1 110.4 %collective-permute-start.8 = (bf16[256,2048]{1,0:T(8,128)(2,1)}, bf16[256,2048]{1,0:T(8,128)(2,1)}, u32[]{:S(2)}, u32[]{:S(2)}) collective-permute-start(bf16[256,2048]{1,0:T(8,128)(2,1)} %param.17), channel_id=1, source_target_pairs={{0,16},{8,24},{16,0},{24,8},{1,17},{9,25},{17,1},{25,9},{2,18},{10... | collective-permute-start | bytes 3145736 | tf_op jit(solution)/shard_map/ppermute | solution.py:174
  105.5 82.6 %all-to-all-start.8 = ((bf16[8,80,2048]{2,1,0:T(8,128)(2,1)}), bf16[8,80,2048]{2,1,0:T(8,128)(2,1)}, u32[]{:S(2)}, u32[]{:S(2)}) async-start(bf16[8,80,2048]{2,1,0:T(8,128)(2,1)} %bitcast.326), calls=%async_computation.8 | async-start | bytes 5242880 | tf_op jit(solution)/shard_map/all_to_all | solution.py:177
  188.0 74.7 %all-to-all-start.10 = ((bf16[8,80,2048]{2,1,0:T(8,128)(2,1)}), bf16[8,80,2048]{2,1,0:T(8,128)(2,1)}, u32[]{:S(2)}, u32[]{:S(2)}) async-start(bf16[8,80,2048]{2,1,0:T(8,128)(2,1)} %bitcast.328), calls=%async_computation.10 | async-start | bytes 5242880 | tf_op jit(solution)/shard_map/all_to_all | solution.py:177
  338.3 128.1 %all-to-all-start.2 = ((bf16[8,80,2048]{2,1,0:T(8,128)(2,1)}), bf16[8,80,2048]{2,1,0:T(8,128)(2,1)}, u32[]{:S(2)}, u32[]{:S(2)}) async-start(bf16[8,80,2048]{2,1,0:T(8,128)(2,1)} %bitcast.329), calls=%async_computation.2 | async-start | bytes 5242880 | tf_op jit(solution)/shard_map/all_to_all | solution.py:177
  348.8 114.0 %collective-permute-start.2 = (bf16[256,2048]{1,0:T(8,128)(2,1)}, bf16[256,2048]{1,0:T(8,128)(2,1)}, u32[]{:S(2)}, u32[]{:S(2)}) collective-permute-start(bf16[256,2048]{1,0:T(8,128)(2,1)} %copy-done.10), channel_id=1, source_target_pairs={{0,16},{8,24},{16,0},{24,8},{1,17},{9,25},{17,1},{25,9},{2,18},{10... | collective-permute-start | bytes 3145736 | tf_op jit(solution)/shard_map/ppermute | solution.py:174
  349.7 121.1 %collective-permute-start.4 = (bf16[256,2048]{1,0:T(8,128)(2,1)}, bf16[256,2048]{1,0:T(8,128)(2,1)}, u32[]{:S(2)}, u32[]{:S(2)}) collective-permute-start(bf16[256,2048]{1,0:T(8,128)(2,1)} %copy-done.10), channel_id=1, source_target_pairs={{0,24},{8,16},{16,8},{24,0},{1,25},{9,17},{17,9},{25,1},{2,26},{10... | collective-permute-start | bytes 3145736 | tf_op jit(solution)/shard_map/ppermute | solution.py:174
  544.6 135.9 %all-gather.10.cloned.1.call-start = ((), (), s32[]{:S(2)}) async-start(), calls=%async_computation.22 | async-start | bytes 1081344 | tf_op jit(solution)/shard_map/all_gather | solution.py:250
  629.1 400.9 %all-gather.12.cloned.1.call-start = ((), (), s32[]{:S(2)}) async-start(), calls=%async_computation.23 | async-start | bytes 9437184 | tf_op jit(solution)/shard_map/all_gather | solution.py:305
  633.4 63.0 %all-to-all-start.18 = ((bf16[256,8,256]{2,0,1:T(8,128)(2,1)}), bf16[256,8,256]{2,0,1:T(8,128)(2,1)}, u32[]{:S(2)}, u32[]{:S(2)}) async-start(bf16[256,8,256]{2,0,1:T(8,128)(2,1)} %bitcast.338), calls=%async_computation.18 | async-start | bytes 2097152 | tf_op jit(solution)/shard_map/all_to_all | solution.py:307
  696.5 49.6 %all-to-all-start.11 = ((bf16[8,80,2048]{2,1,0:T(8,128)(2,1)}), bf16[8,80,2048]{2,1,0:T(8,128)(2,1)}, u32[]{:S(2)}, u32[]{:S(2)}) async-start(bf16[8,80,2048]{2,1,0:T(8,128)(2,1)} %bitcast.349), calls=%async_computation.11 | async-start | bytes 5242880 | tf_op jit(solution)/shard_map/all_to_all | solution.py:177
  833.5 72.2 %collective-permute-start.9 = (bf16[256,2048]{1,0:T(8,128)(2,1)}, bf16[256,2048]{1,0:T(8,128)(2,1)}, u32[]{:S(2)}, u32[]{:S(2)}) collective-permute-start(bf16[256,2048]{1,0:T(8,128)(2,1)} %convolution_convert_fusion.16), channel_id=1, source_target_pairs={{0,16},{8,24},{16,0},{24,8},{1,17},{9,25},{17,1},{25,9},{2,18},{10... | collective-permute-start | bytes 3145736 | tf_op jit(solution)/shard_map/ppermute | solution.py:174
  839.6 66.2 %collective-permute-start.11 = (bf16[256,2048]{1,0:T(8,128)(2,1)}, bf16[256,2048]{1,0:T(8,128)(2,1)}, u32[]{:S(2)}, u32[]{:S(2)}) collective-permute-start(bf16[256,2048]{1,0:T(8,128)(2,1)} %convolution_convert_fusion.15), channel_id=1, source_target_pairs={{0,24},{8,16},{16,8},{24,0},{1,25},{9,17},{17,9},{25,1},{2,26},{10... | collective-permute-start | bytes 3145736 | tf_op jit(solution)/shard_map/ppermute | solution.py:174
  863.1 104.5 %all-to-all-start.19 = ((bf16[256,8,512]{2,0,1:T(8,128)(2,1)}), bf16[256,8,512]{2,0,1:T(8,128)(2,1)}, u32[]{:S(2)}, u32[]{:S(2)}) async-start(bf16[256,8,512]{2,0,1:T(8,128)(2,1)} %copy.265), calls=%async_computation.19 | async-start | bytes 4194304 | tf_op jit(solution)/shard_map/all_to_all | solution.py:306
  867.5 266.0 %all-gather.14.cloned.1.call-start = ((), (), s32[]{:S(2)}) async-start(), calls=%async_computation.24 | async-start | bytes 9437184 | tf_op jit(solution)/shard_map/all_gather | solution.py:303
  967.5 48.8 %all-to-all-start.16 = ((bf16[256,8,640]{0,2,1:T(8,128)(2,1)}), bf16[256,8,640]{0,2,1:T(8,128)(2,1)}, u32[]{:S(2)}, u32[]{:S(2)}) async-start(bf16[256,8,640]{0,2,1:T(8,128)(2,1)} %pad_maximum_fusion.1), calls=%async_computation.16 | async-start | bytes 5242880 | tf_op jit(solution)/shard_map/all_to_all | solution.py:334
  1128.7 55.6 %all-to-all-start.7 = ((bf16[8,80,2048]{2,1,0:T(8,128)(2,1)}), bf16[8,80,2048]{2,1,0:T(8,128)(2,1)}, u32[]{:S(2)}, u32[]{:S(2)}) async-start(bf16[8,80,2048]{2,1,0:T(8,128)(2,1)} %bitcast.343), calls=%async_computation.7 | async-start | bytes 5242880 | tf_op jit(solution)/shard_map/all_to_all | solution.py:177
  1133.1 290.0 %all-reduce.10.cloned.1.call-start = ((), (), s32[]{:S(2)}) async-start(), calls=%async_computation.25 | async-start | bytes 9568256 | tf_op jit(solution)/shard_map/psum | solution.py:349
  1152.2 222.1 %collective-permute-start.1 = (bf16[256,2048]{1,0:T(8,128)(2,1)}, bf16[256,2048]{1,0:T(8,128)(2,1)}, u32[]{:S(2)}, u32[]{:S(2)}) collective-permute-start(bf16[256,2048]{1,0:T(8,128)(2,1)} %convolution_convert_fusion.20), channel_id=1, source_target_pairs={{0,8},{8,0},{16,24},{24,16},{1,9},{9,1},{17,25},{25,17},{2,10},{10... | collective-permute-start | bytes 3145736 | tf_op jit(solution)/shard_map/ppermute | solution.py:174
  1183.4 190.9 %collective-permute-start.3 = (bf16[256,2048]{1,0:T(8,128)(2,1)}, bf16[256,2048]{1,0:T(8,128)(2,1)}, u32[]{:S(2)}, u32[]{:S(2)}) collective-permute-start(bf16[256,2048]{1,0:T(8,128)(2,1)} %convolution_convert_fusion.19), channel_id=1, source_target_pairs={{0,16},{8,24},{16,0},{24,8},{1,17},{9,25},{17,1},{25,9},{2,18},{10... | collective-permute-start | bytes 3145736 | tf_op jit(solution)/shard_map/ppermute | solution.py:174
  1184.3 190.0 %all-to-all-start.1 = ((bf16[8,80,2048]{2,1,0:T(8,128)(2,1)}), bf16[8,80,2048]{2,1,0:T(8,128)(2,1)}, u32[]{:S(2)}, u32[]{:S(2)}) async-start(bf16[8,80,2048]{2,1,0:T(8,128)(2,1)} %bitcast.344), calls=%async_computation.1 | async-start | bytes 5242880 | tf_op jit(solution)/shard_map/all_to_all | solution.py:177
  1192.9 181.4 %collective-permute-start.5 = (bf16[256,2048]{1,0:T(8,128)(2,1)}, bf16[256,2048]{1,0:T(8,128)(2,1)}, u32[]{:S(2)}, u32[]{:S(2)}) collective-permute-start(bf16[256,2048]{1,0:T(8,128)(2,1)} %convolution_convert_fusion.18), channel_id=1, source_target_pairs={{0,24},{8,16},{16,8},{24,0},{1,25},{9,17},{17,9},{25,1},{2,26},{10... | collective-permute-start | bytes 3145736 | tf_op jit(solution)/shard_map/ppermute | solution.py:174
  (132 other events, 4471.3 us)
Sparse Core Ops, SparseCore 0:
  11.4 124.9 all-gather.5
  138.3 133.4 all-gather.7
  629.2 51.2 all-gather.9
  682.8 74.0 all-gather.11
  932.9 97.9 all-gather.13
  1143.5 279.6 all-reduce.9

commit v2 on v1

--- a/solution.py
+++ b/solution.py
@@ -130,6 +130,11 @@
     return jnp.where(hit, slots, -1.0)
 
 
+def return_order(n_exp):
+    half = max(1, n_exp // 2)
+    return list(range(half, n_exp)) + list(range(half))
+
+
 def dot32(left, right):
     return jnp.dot(left, right, preferred_element_type=jnp.float32)
 
@@ -140,7 +145,7 @@
     )
 
 
-def body(
+def layer(
     tokens,
     cotangent,
     routes,
@@ -163,52 +168,59 @@
     top_k = routes.shape[1]
     n_exp = lax.axis_size("expert")
     n_fsdp = lax.axis_size("fsdp")
-    everyone = ("expert", "fsdp")
     cap = max(2, token_count * top_k * 5 // (4 * experts))
     plane = lax.axis_index("expert")
-    column = lax.axis_index("fsdp")
     rel = range(n_exp)
+    back_order = return_order(n_exp)
     bf = jnp.bfloat16
 
     def across(value, r):
-        return lax.ppermute(value, "expert", [(i, i ^ r) for i in range(n_exp)]) if r else value
-
-    def in_plane(value):
-        return lax.all_to_all(value, "fsdp", split_axis=0, concat_axis=0, tiled=True)
-
-    routes_t = routes.T
-    routes_all = lax.all_gather(routes_t, everyone, axis=0, tiled=True)
-    routes_all = routes_all.reshape(n_exp, n_fsdp, top_k, token_count)
+        return lax.ppermute(value, "expert", [(i, i ^ r) for i in range(n_exp)])
+
+    def in_plane(value, split=0, concat=0):
+        return lax.all_to_all(value, "fsdp", split_axis=split, concat_axis=concat, tiled=True)
+
+    def gathered(value):
+        return lax.all_gather(value, "fsdp", axis=0, tiled=True)
+
+    def with_notes(rows, notes):
+        flat = jnp.concatenate([note.reshape(-1) for note in notes]).astype(bf)
+        lines = -(-flat.shape[0] // (8 * width)) * 8
+        flat = jnp.pad(flat, (0, lines * width - flat.shape[0]))
+        return jnp.concatenate([rows, flat.reshape(lines, width)], axis=0)
+
+    def note_of(rows, number):
+        first = token_count * width + number * n_fsdp * token_count
+        line, rest = first // width, n_fsdp * token_count
+        lines = -(-rest // width)
+        if first % width == 0 and rest % width == 0:
+            flat = rows[line : line + lines].reshape(-1)
+        else:
+            flat = rows.reshape(-1)[first : first + rest]
+        return flat.astype(jnp.float32).reshape(n_fsdp, token_count)
+
+    def halves(value):
+        high = value.astype(bf)
+        return [high, (value - high.astype(jnp.float32)).astype(bf)]
+
     planes_rel = jnp.arange(n_exp, dtype=jnp.int32) ^ plane
-    routes_rel = jnp.take(routes_all, planes_rel, axis=0)
-    routes_col = lax.dynamic_index_in_dim(routes_rel, column, 1, keepdims=False)
-    plane_experts = plane * n_fsdp + jnp.arange(n_fsdp, dtype=jnp.int32)
+    own_places = route_places(routes.T, jnp.arange(experts, dtype=jnp.int32))
+    places_rel = jnp.take(own_places.reshape(n_exp, n_fsdp, token_count), planes_rel, axis=0)
     slot_ids = jnp.arange(cap, dtype=jnp.int32).astype(jnp.float32)
-    col_places = route_places(routes_col, plane_experts)
-    picks = (col_places[:, :, None, :] == slot_ids[:, None]).astype(bf)
-    picks = picks.reshape(n_exp, n_fsdp * cap, token_count)
-    own_expert = plane * n_fsdp + column
-    expert_places = route_places(routes_rel, own_expert[None])[:, :, 0, :]
-    own_places = route_places(routes_t, jnp.arange(experts, dtype=jnp.int32))
-
-    def dispatch(value):
-        out = []
-        for r in rel:
-            rows = dot32(picks[r], across(value, r)).astype(bf)
-            out.append(in_plane(rows.reshape(n_fsdp, cap, width)).reshape(n_fsdp * cap, width))
-        return out
-
-    def combine(parts):
-        total = None
-        for r in rel:
-            back = in_plane(parts[r].reshape(n_fsdp, cap, width)).reshape(n_fsdp * cap, width)
-            summed = first_dot(picks[r], back)
-            if r:
-                summed = across(summed.astype(bf), r).astype(jnp.float32)
-            total = summed if total is None else total + summed
-        return total
-
-    grad_rows = dispatch(cotangent)
+    col_places, picks, grad_rows = [], [], []
+    for r in rel:
+        rows = cotangent
+        places = places_rel[0]
+        if r:
+            rows = across(with_notes(cotangent, [places_rel[r]]), r)
+            places = note_of(rows, 0)
+            rows = rows[:token_count]
+        pick = (places[:, None, :] == slot_ids[:, None]).astype(bf)
+        pick = pick.reshape(n_fsdp * cap, token_count)
+        col_places.append(places)
+        picks.append(pick)
+        rows = dot32(pick, rows).astype(bf).reshape(n_fsdp, cap, width)
+        grad_rows.append(in_plane(rows).reshape(n_fsdp * cap, width))
 
     position, allowed = layout(seq_lens[0], token_count)
     rotary_angles = angles_of(position)
@@ -219,10 +231,12 @@
     k_cols = wk.shape[1]
     pad = -experts % 128
     packed = jnp.concatenate([wq, wk, wv, jnp.pad(wr, ((0, 0), (0, pad)))], axis=1)
-    w_in = lax.all_gather(packed, "fsdp", axis=0, tiled=True)
+    w_in = gathered(packed)
     wr_all = w_in[:, q_cols + 2 * k_cols : q_cols + 2 * k_cols + experts]
-    wo_all = lax.all_gather(wo, "fsdp", axis=0, tiled=True)
-    proj = dot32(x_norm, w_in)
+    wo_all = gathered(wo)
+    x_in, *early = lax.optimization_barrier((x_norm, *grad_rows[: n_exp - 1]))
+    grad_rows = early + grad_rows[n_exp - 1 :]
+    proj = dot32(x_in, w_in)
     q_proj = proj[:, :q_cols]
     key_projection = proj[:, q_cols : q_cols + k_cols]
     value_projection = proj[:, q_cols + k_cols : q_cols + 2 * k_cols]
@@ -235,11 +249,11 @@
     key_head_rows = key_f.astype(bf)
     value_rows = value_projection.reshape(token_count, KEY_VALUE_HEADS, HEAD_SIZE).astype(bf)
     head_output, log_total = attend(query_rows, key_head_rows, value_rows, allowed)
+    head_output, grad_rows[-1] = lax.optimization_barrier((head_output, grad_rows[-1]))
     resid = x_f + dot32(head_output, wo_all)
     moe_norm, moe_back = jax.vjp(root_mean_norm, resid, moe_gain)
     moe_in = moe_norm.astype(bf)
 
-    flat_in = dispatch(moe_in)
     logits = lax.dot_general(
         wr_all, moe_in, (((0,), (1,)), ((), ())), preferred_element_type=jnp.float32
     )
@@ -247,14 +261,27 @@
     top_logit = jnp.max(jnp.where(chosen, logits, -jnp.inf), axis=0, keepdims=True)
     raised = jnp.where(chosen, jnp.exp(jnp.where(chosen, logits - top_logit, 0.0)), 0.0)
     gates = raised / jnp.sum(raised, axis=0, keepdims=True)
-    gates_all = lax.all_gather(gates, everyone, axis=0, tiled=True)
-    gates_all = gates_all.reshape(n_exp, n_fsdp, experts, token_count)
-    gate_own = lax.dynamic_index_in_dim(gates_all, own_expert, 2, keepdims=False)
-    gate_own = jnp.take(gate_own, planes_rel, axis=0)
-    slot_gates = jnp.sum(
-        jnp.where(expert_places[:, :, None, :] == slot_ids[:, None], gate_own[:, :, None, :], 0.0),
-        axis=3,
-    )
+    gates_rel = jnp.take(gates.reshape(n_exp, n_fsdp, token_count), planes_rel, axis=0)
+    flat_in, slot_gates = [], []
+    for r in rel:
+        rows = moe_in
+        gate_rows = gates_rel[0]
+        if r:
+            rows = across(with_notes(moe_in, halves(gates_rel[r])), r)
+            gate_rows = note_of(rows, 0) + note_of(rows, 1)
+            rows = rows[:token_count]
+        rows = dot32(picks[r], rows).astype(bf).reshape(n_fsdp, cap, width)
+        flat_in.append(in_plane(rows).reshape(n_fsdp * cap, width))
+        found = col_places[r][:, None, :] == slot_ids[:, None]
+        slot_gates.append(jnp.sum(jnp.where(found, gate_rows[:, None, :], 0.0), axis=2))
+    half = max(1, n_exp // 2)
+    slot_gates = [
+        part
+        for first in range(0, n_exp, half)
+        for part in in_plane(jnp.stack(slot_gates[first : first + half], axis=1))
+        .transpose(1, 0, 2)
+        .reshape(half, n_fsdp * cap, 1)
+    ]
     gate_mat = w_gate[0]
     up_mat = w_up[0]
     down_mat = w_down[0]
@@ -263,7 +290,7 @@
         gate_pre = dot32(flat_in[r], gate_mat)
         up_pre = dot32(flat_in[r], up_mat)
         d_plain = back_dot(grad_rows[r], down_mat)
-        scale = slot_gates[r].reshape(-1, 1)
+        scale = slot_gates[r]
         sigma = jax.nn.sigmoid(gate_pre)
         active = gate_pre * sigma
         hidden = active * up_pre
@@ -279,14 +306,21 @@
         hid_parts.append(hidden_scaled)
         dg_parts.append(d_gate_pre)
         du_parts.append(d_up_pre)
-    d_moe_in = combine(back_parts)
-    gate_grads = jnp.take(jnp.stack(gate_grads), planes_rel, axis=0)
-    gate_grads = lax.all_gather(gate_grads.reshape(n_exp * n_fsdp, cap), everyone, axis=0, tiled=True)
-    gate_grads = gate_grads.reshape(experts, n_exp * n_fsdp, cap)
-    gate_grads = lax.dynamic_index_in_dim(gate_grads, own_expert, 1, keepdims=False)
-    d_gates = jnp.sum(
-        jnp.where(own_places[:, None, :] == slot_ids[:, None], gate_grads[:, :, None], 0.0), axis=1
-    )
+    gate_grads = in_plane(jnp.stack(gate_grads, axis=1))
+    d_gates = [None] * n_exp
+    d_moe_in = None
+    for r in back_order:
+        back = in_plane(back_parts[r].reshape(n_fsdp, cap, width))
+        summed = first_dot(picks[r], back.reshape(n_fsdp * cap, width))
+        found = col_places[r][:, None, :] == slot_ids[:, None]
+        gate_part = jnp.sum(jnp.where(found, gate_grads[:, r, :, None], 0.0), axis=1)
+        if r:
+            rows = across(with_notes(summed.astype(bf), halves(gate_part)), r)
+            gate_part = note_of(rows, 0) + note_of(rows, 1)
+            summed = rows[:token_count].astype(jnp.float32)
+        d_moe_in = summed if d_moe_in is None else d_moe_in + summed
+        d_gates[r] = gate_part
+    d_gates = jnp.take(jnp.stack(d_gates), planes_rel, axis=0).reshape(experts, token_count)
     d_logits = gates * (d_gates - jnp.sum(gates * d_gates, axis=0, keepdims=True))
     d_moe_in = d_moe_in + lax.dot_general(
         d_logits,
@@ -300,11 +334,18 @@
     d_resid = d_out + d_resid_norm
     d_attn = d_resid.astype(bf)
 
-    d_attn_all = lax.all_gather(d_attn, "fsdp", axis=0, tiled=True)
-    d_logits_all = lax.all_gather(d_logits, "fsdp", axis=0, tiled=True)
-    x_norm_all = lax.all_gather(x_norm, "fsdp", axis=0, tiled=True)
-    heads_cols = lax.all_to_all(head_output, "fsdp", split_axis=1, concat_axis=0, tiled=True)
-    moe_cols = lax.all_to_all(moe_in, "fsdp", split_axis=1, concat_axis=0, tiled=True)
+    d_attn_all = gathered(d_attn)
+    x_norm_all = gathered(x_norm)
+    heads_cols = in_plane(head_output, 1, 0)
+    grad_router = lax.dot_general(
+        d_logits,
+        moe_in.astype(jnp.float32),
+        (((1,), (0,)), ((), ())),
+        precision=lax.Precision.HIGHEST,
+        preferred_element_type=jnp.float32,
+    )
+    grad_router = grad_router.reshape(experts, n_fsdp, width // n_fsdp).transpose(1, 0, 2)
+    grad_router = jnp.sum(in_plane(grad_router), axis=0).T
     head_gradient = back_dot(d_attn, wo_all).astype(bf)
     d_query, d_key, value_gradient = attend_back(
         query_rows, key_head_rows, value_rows, head_output, head_gradient, log_total, allowed
@@ -331,21 +372,14 @@
         ],
         axis=2,
     ).reshape(token_count, -1)
-    d_cols = lax.all_to_all(d_cols, "fsdp", split_axis=1, concat_axis=0, tiled=True)
+    d_cols = in_plane(d_cols, 1, 0)
     grad_in = first_dot(x_norm_all, d_cols).astype(bf)
-    grad_in = lax.all_to_all(grad_in, "fsdp", split_axis=0, concat_axis=1, tiled=True)
-    d_logits_all = d_logits_all.reshape(n_fsdp, experts, token_count)
-    d_logits_all = jnp.transpose(d_logits_all, (1, 0, 2)).reshape(experts, n_fsdp * token_count)
-    grad_router = lax.dot_general(
-        moe_cols.astype(jnp.float32),
-        d_logits_all,
-        (((0,), (1,)), ((), ())),
-        precision=lax.Precision.HIGHEST,
-        preferred_element_type=jnp.float32,
-    )
-    grad_outproj = lax.psum(grad_outproj.astype(bf), "expert").astype(jnp.float32)
+    grad_in = in_plane(grad_in, 0, 1)
+    grad_outproj = lax.psum(grad_outproj.astype(bf), "expert")
     grad_router = jnp.pad(grad_router.astype(bf), ((0, 0), (0, pad)))
     grad_rows_in = jnp.concatenate([grad_in, grad_router], axis=1)
+    grad_rows_in, grad_outproj = lax.optimization_barrier((grad_rows_in, grad_outproj))
+    grad_outproj = grad_outproj.astype(jnp.float32)
     grad_rows_in = lax.psum(grad_rows_in, "expert").astype(jnp.float32)
     in_cols = n_fsdp * (q_part + 2 * k_part)
     split = grad_rows_in[:, :in_cols].reshape(-1, n_fsdp, q_part + 2 * k_part)
@@ -358,8 +392,25 @@
     grad_gate = first_dot(rows_in, jnp.concatenate(dg_parts, axis=0))
     grad_up = first_dot(rows_in, jnp.concatenate(du_parts, axis=0))
     grad_down = first_dot(jnp.concatenate(hid_parts, axis=0), jnp.concatenate(grad_rows, axis=0))
-    layer_out = (resid + combine(out_parts)).astype(bf)
-    gain_sums = lax.psum((d_attn_gain, d_q_gain, d_k_gain, d_moe_gain), everyone)
+    mixed = resid
+    for r in back_order:
+        back = in_plane(out_parts[r].reshape(n_fsdp, cap, width))
+        summed = first_dot(picks[r], back.reshape(n_fsdp * cap, width))
+        if r:
+            summed = across(summed.astype(bf), r).astype(jnp.float32)
+        mixed = mixed + summed
+    layer_out = mixed.astype(bf)
+    gains = [d_attn_gain, d_q_gain, d_k_gain, d_moe_gain]
+    sizes = [gain.shape[0] for gain in gains]
+    gain_rows = jnp.concatenate(gains).reshape(-1, HEAD_SIZE)
+    gain_rows = jnp.broadcast_to(gain_rows, (n_fsdp,) + gain_rows.shape)
+    gain_rows = jnp.sum(in_plane(gain_rows), axis=0)
+    by_plane = jnp.stack([across(gain_rows, r) if r else gain_rows for r in rel])
+    gain_rows = jnp.sum(jnp.take(by_plane, planes_rel, axis=0), axis=0).reshape(-1)
+    gain_sums, at = [], 0
+    for size in sizes:
+        gain_sums.append(gain_rows[at : at + size])
+        at += size
     return (
         layer_out,
         d_tokens,
@@ -413,4 +464,4 @@
         P(("expert", "fsdp"), None, None),
         P(("expert", "fsdp"), None, None),
     )
-    return jax.shard_map(body, mesh=mesh, in_specs=in_specs, out_specs=out_specs, check_vma=False)
+    return jax.shard_map(layer, mesh=mesh, in_specs=in_specs, out_specs=out_specs, check_vma=False)

time: 1460 us -> 1330 us (0.911)
  blocking collectives: 301 us -> 0 us
  waiting for transfers between devices: 490 us -> 648 us
  other arithmetic: 80.3 us -> 100 us
    psum x1 -> x0, blocking collectives: 163 us -> none  [body(): lax.psum((d_attn_gain, d_q_gain, d_k_gain, d_moe_gain), everyone)]
    all_gather x3 -> x0, blocking collectives: 138 us -> none  [the longest x1 81.3 us: body(): routes_all = lax.all_gather(routes_t, everyone, axis=0, tiled=True)]
    ppermute x12 -> x15, waiting for transfers between devices: 163 us -> 254 us  [across(): return lax.ppermute(value, 'expert', [(i, i ^ r) for i in range(n_exp)])]
    all_to_all x20 -> x24, waiting for transfers between devices: 231 us -> 306 us  [in_plane(): lax.all_to_all(value, 'fsdp', split_axis=split, concat_axis=concat, tiled...]
    all_gather x5 -> x4, waiting for transfers between devices: 54.4 us -> 0.04 us  [gathered(): return lax.all_gather(value, 'fsdp', axis=0, tiled=True)]
    psum x1 -> x2, waiting for transfers between devices: 40.7 us -> 87 us  [the longest x1 64.8 us: layer(): grad_rows_in = lax.psum(grad_rows_in, 'expert').astype(jnp.float32)]
    ppermute x12 -> x15, starting transfers between devices: 56.3 us -> 40.7 us  [across(): return lax.ppermute(value, 'expert', [(i, i ^ r) for i in range(n_exp)])]
    convert_element_type x11 -> x22, other arithmetic: 34.5 us -> 40.3 us  [the longest x4 17.3 us: layer(): d_up_pre = (d_hidden * active).astype(bf)]
  transfers between devices with their start and end apart: 38 -> 45, of which waited for: 21 -> 26; matrix products, arithmetic and copies ran while one was open for 30% -> 34% of each run, Pallas kernels for 0% -> 0%
where the time goes in v2:
time: 1330 us; the launch traced here: 1320 us
  waiting for transfers between devices  648 us (49%)
  matrix products  307 us (23%)
  starting transfers between devices  146 us (11%)
  local copies, waits for them, and re-layouts  101 us (8%)
  other arithmetic  100 us (8%)
  between operations  16.6 us (1%)
    all_to_all x24, waiting for transfers between devices, in_plane(): lax.all_to_all(value, 'fsdp', split_axis=split, concat_axis=concat, tiled...  306 us
    ppermute x15, waiting for transfers between devices, across(): return lax.ppermute(value, 'expert', [(i, i ^ r) for i in range(n_exp)])  254 us
    dot_general x22, matrix products, dot32(): return jnp.dot(left, right, preferred_element_type=jnp.float32)  107 us
    all_to_all x24, starting transfers between devices, in_plane(): lax.all_to_all(value, 'fsdp', split_axis=split, concat_axis=concat, tiled...  105 us
    dot_general x13, matrix products, first_dot(): lax.dot_general(left, right, (((0,), (0,)), ((), ())), preferred_element_...  94.3 us
    dot_general x14, matrix products, back_dot(): lax.dot_general(left, right, (((1,), (1,)), ((), ())), preferred_element_...  77.5 us
    psum x1, waiting for transfers between devices, layer(): grad_rows_in = lax.psum(grad_rows_in, 'expert').astype(jnp.float32)  64.8 us
    ppermute x15, starting transfers between devices, across(): return lax.ppermute(value, 'expert', [(i, i ^ r) for i in range(n_exp)])  40.7 us
  transfers between devices with their start and end apart: 45, of which 26 were waited for; matrix products, arithmetic and copies ran while one was open for 34% of the time, Pallas kernels for 0%

profile of v2, /device:TPU:0, one launch (start us, length us, event | category | flops | bytes accessed | tf_op | source)
XLA Modules:
  0.0 1318.2 jit_solution(14205500576693026975)
XLA Ops:
  22.5 24.5 %collective-permute-done.2 = bf16[264,2048]{1,0:T(8,128)(2,1)} collective-permute-done((bf16[264,2048]{1,0:T(8,128)(2,1)}, bf16[264,2048]{1,0:T(8,128)(2,1)}, u32[]{:S(2)}, u32[]{:S(2)}) %collective-permute-start.2) | collective-permute-done | bytes 1081376 | tf_op jit(solution)/shard_map/ppermute | solution.py:178
  47.8 22.5 %collective-permute-done = bf16[264,2048]{1,0:T(8,128)(2,1)} collective-permute-done((bf16[264,2048]{1,0:T(8,128)(2,1)}, bf16[264,2048]{1,0:T(8,128)(2,1)}, u32[]{:S(2)}, u32[]{:S(2)}) %collective-permute-start) | collective-permute-done | bytes 1081376 | tf_op jit(solution)/shard_map/ppermute | solution.py:178
  71.1 43.6 %collective-permute-done.1 = bf16[264,2048]{1,0:T(8,128)(2,1)} collective-permute-done((bf16[264,2048]{1,0:T(8,128)(2,1)}, bf16[264,2048]{1,0:T(8,128)(2,1)}, u32[]{:S(2)}, u32[]{:S(2)}) %collective-permute-start.1) | collective-permute-done | bytes 1081376 | tf_op jit(solution)/shard_map/ppermute | solution.py:178
  128.8 48.3 %all-to-all-done = bf16[8,80,2048]{2,1,0:T(8,128)(2,1)} async-done(((bf16[8,80,2048]{2,1,0:T(8,128)(2,1)}), bf16[8,80,2048]{2,1,0:T(8,128)(2,1)}, u32[]{:S(2)}, u32[]{:S(2)}) %all-to-all-start) | async-done | bytes 2621472 | tf_op jit(solution)/shard_map/all_to_all | solution.py:181
  185.8 55.8 %all-to-all-done.1 = bf16[8,80,2048]{2,1,0:T(8,128)(2,1)} async-done(((bf16[8,80,2048]{2,1,0:T(8,128)(2,1)}), bf16[8,80,2048]{2,1,0:T(8,128)(2,1)}, u32[]{:S(2)}, u32[]{:S(2)}) %all-to-all-start.1) | async-done | bytes 2621472 | tf_op jit(solution)/shard_map/all_to_all | solution.py:181
  258.8 28.2 %all-to-all-done.2 = bf16[8,80,2048]{2,1,0:T(8,128)(2,1)} async-done(((bf16[8,80,2048]{2,1,0:T(8,128)(2,1)}), bf16[8,80,2048]{2,1,0:T(8,128)(2,1)}, u32[]{:S(2)}, u32[]{:S(2)}) %all-to-all-start.2) | async-done | bytes 2621472 | tf_op jit(solution)/shard_map/all_to_all | solution.py:181
  388.2 27.0 %collective-permute-done.4 = bf16[264,2048]{1,0:T(8,128)(2,1)S(1)} collective-permute-done((bf16[264,2048]{1,0:T(8,128)(2,1)S(1)}, bf16[264,2048]{1,0:T(8,128)(2,1)S(1)}, u32[]{:S(2)}, u32[]{:S(2)}) %collective-permute-start.4) | collective-permute-done | bytes 1081376 | tf_op jit(solution)/shard_map/ppermute | solution.py:178
  422.9 18.4 %collective-permute-start.3 = (bf16[264,2048]{1,0:T(8,128)(2,1)}, bf16[264,2048]{1,0:T(8,128)(2,1)}, u32[]{:S(2)}, u32[]{:S(2)}) collective-permute-start(bf16[264,2048]{1,0:T(8,128)(2,1)} %get-tuple-element.193), channel_id=1, source_target_pairs={{0,16},{8,24},{16,0},{24,8},{1,17},{9,25},{17,1},{25,9},{2,18},{10... | collective-permute-start | bytes 3244040 | tf_op jit(solution)/shard_map/ppermute | solution.py:178
  460.5 28.6 %collective-permute-done.3 = bf16[264,2048]{1,0:T(8,128)(2,1)} collective-permute-done((bf16[264,2048]{1,0:T(8,128)(2,1)}, bf16[264,2048]{1,0:T(8,128)(2,1)}, u32[]{:S(2)}, u32[]{:S(2)}) %collective-permute-start.3) | collective-permute-done | bytes 1081376 | tf_op jit(solution)/shard_map/ppermute | solution.py:178
  525.3 14.4 %all-to-all-done.4 = bf16[8,80,2048]{2,1,0:T(8,128)(2,1)} async-done(((bf16[8,80,2048]{2,1,0:T(8,128)(2,1)}), bf16[8,80,2048]{2,1,0:T(8,128)(2,1)}, u32[]{:S(2)}, u32[]{:S(2)}) %all-to-all-start.4) | async-done | bytes 2621472 | tf_op jit(solution)/shard_map/all_to_all | solution.py:181
  662.2 20.8 %all-to-all-done.16 = bf16[8,80,2048]{2,1,0:T(8,128)(2,1)} async-done(((bf16[8,80,2048]{2,1,0:T(8,128)(2,1)}), bf16[8,80,2048]{2,1,0:T(8,128)(2,1)}, u32[]{:S(2)}, u32[]{:S(2)}) %all-to-all-start.16) | async-done | bytes 2621472 | tf_op jit(solution)/shard_map/all_to_all | solution.py:181
  698.9 20.7 %all-to-all-done.14 = bf16[8,80,2048]{2,1,0:T(8,128)(2,1)} async-done(((bf16[8,80,2048]{2,1,0:T(8,128)(2,1)}), bf16[8,80,2048]{2,1,0:T(8,128)(2,1)}, u32[]{:S(2)}, u32[]{:S(2)}) %all-to-all-start.14) | async-done | bytes 2621472 | tf_op jit(solution)/shard_map/all_to_all | solution.py:181
  738.0 18.5 %all-to-all-done.18 = bf16[8,80,2048]{2,1,0:T(8,128)(2,1)} async-done(((bf16[8,80,2048]{2,1,0:T(8,128)(2,1)}), bf16[8,80,2048]{2,1,0:T(8,128)(2,1)}, u32[]{:S(2)}, u32[]{:S(2)}) %all-to-all-start.18) | async-done | bytes 2621472 | tf_op jit(solution)/shard_map/all_to_all | solution.py:181
  780.8 12.3 all-to-all-done.17
  802.9 58.8 %collective-permute-done.9 = bf16[264,2048]{1,0:T(8,128)(2,1)} collective-permute-done((bf16[264,2048]{1,0:T(8,128)(2,1)}, bf16[264,2048]{1,0:T(8,128)(2,1)}, u32[]{:S(2)}, u32[]{:S(2)}) %collective-permute-start.9) | collective-permute-done | bytes 1081376 | tf_op jit(solution)/shard_map/ppermute | solution.py:178
  873.7 14.6 %fusion.42 = f32[1,2048,768]{2,1,0:T(8,128)} fusion(bf16[640,768]{1,0:T(8,128)(2,1)} %copy-done.62, bf16[640,768]{1,0:T(8,128)(2,1)} %copy-done.63, bf16[640,768]{1,0:T(8,128)(2,1)} %copy-done.64, bf16[640,768]{1,0:T(8,128)(2,1)} %copy-done.65, bf16[640,2048]{1,0:T(8,128)(2,1)} %bitcast.39, bf16[640,2048]{1,0:T(8,128)(2,1)} %bitcast.29, ...), kind=kOutput, calls=%fused_computation.69 | convolution fusion | flops 8110735360 | bytes 20709376 | tf_op jit(solution)/shard_map/dot_general | solution.py:143
  933.9 21.5 %all-to-all-done.8 = bf16[8,80,2048]{2,1,0:T(8,128)(2,1)} async-done(((bf16[8,80,2048]{2,1,0:T(8,128)(2,1)}), bf16[8,80,2048]{2,1,0:T(8,128)(2,1)}, u32[]{:S(2)}, u32[]{:S(2)}) %all-to-all-start.8) | async-done | bytes 2621472 | tf_op jit(solution)/shard_map/all_to_all | solution.py:181
  975.9 16.3 %all-to-all-done.6 = bf16[8,80,2048]{2,1,0:T(8,128)(2,1)} async-done(((bf16[8,80,2048]{2,1,0:T(8,128)(2,1)}), bf16[8,80,2048]{2,1,0:T(8,128)(2,1)}, u32[]{:S(2)}, u32[]{:S(2)}) %all-to-all-start.6) | async-done | bytes 2621472 | tf_op jit(solution)/shard_map/all_to_all | solution.py:181
  997.0 14.2 %fusion.39 = f32[1,2048,768]{2,1,0:T(8,128)} fusion(bf16[640,768]{1,0:T(8,128)(2,1)} %copy-done.58, bf16[640,768]{1,0:T(8,128)(2,1)} %copy-done.59, bf16[640,768]{1,0:T(8,128)(2,1)} %copy-done.60, bf16[640,768]{1,0:T(8,128)(2,1)} %copy-done.61, bf16[640,2048]{1,0:T(8,128)(2,1)} %bitcast.39, bf16[640,2048]{1,0:T(8,128)(2,1)} %bitcast.29, ...), kind=kOutput, calls=%fused_computation.68 | convolution fusion | flops 8110735360 | bytes 20709376 | tf_op jit(solution)/shard_map/dot_general | solution.py:143
  1084.8 14.3 %fusion.45 = f32[1,768,2048]{2,1,0:T(8,128)} fusion(bf16[640,2048]{1,0:T(8,128)(2,1)} %bitcast.26, bf16[640,2048]{1,0:T(8,128)(2,1)} %bitcast.11, bf16[640,2048]{1,0:T(8,128)(2,1)} %bitcast.8, bf16[640,2048]{1,0:T(8,128)(2,1)} %bitcast.5, bf16[640,768]{1,0:T(8,128)(2,1)} %get-tuple-element.184, bf16[640,768]{1,0:T(8,128)(2,1)} %get-tuple-element.181, ...), kind=kOutput, calls=%fused_computation.70 | convolution fusion | flops 8110735360 | bytes 20709376 | tf_op jit(solution)/shard_map/dot_general | solution.py:143
  1099.1 48.9 %collective-permute-done.5 = bf16[256,2048]{1,0:T(8,128)(2,1)} collective-permute-done((bf16[256,2048]{1,0:T(8,128)(2,1)}, bf16[256,2048]{1,0:T(8,128)(2,1)}, u32[]{:S(2)}, u32[]{:S(2)}) %collective-permute-start.5) | collective-permute-done | bytes 1048608 | tf_op jit(solution)/shard_map/ppermute | solution.py:178
  1162.5 22.2 %all-reduce.18.cloned.1.call-done = bf16[512,2048]{1,0:T(8,128)(2,1)} async-done(((bf16[512,2048]{1,0:T(8,128)(2,1)}), bf16[512,2048]{1,0:T(8,128)(2,1)}) %all-reduce.18.cloned.1.call-update) | async-done | bytes 2097168 | tf_op jit(solution)/shard_map/psum | solution.py:378
  1184.9 18.2 %fusion.108 = (f32[2048]{0:T(1024)S(1)}, f32[256]{0:T(256)S(1)}, f32[256,2048]{1,0:T(8,128)}) fusion(bf16[256,2048]{1,0:T(8,128)(2,1)} %param.18, f32[256]{0:T(256)S(1)} %copy-done.111, f32[2048]{0:T(1024)S(1)} %copy-done.95, bf16[2048,5248]{1,0:T(8,128)(2,1)} %all-gather.5.cloned.1.call-done, bf16[256,512]{0,1:T(8,128)(2,1)S(1)} %bitcast.410, ...), kind=kOutput, calls=%fused_computation.154 | convolution fusion | flops 5517342720 | bytes 27291904 | tf_op jit(solution)/shard_map/dot_general | solution.py:63
  1229.6 64.8 %all-reduce.20.cloned.1.call-done = bf16[256,5248]{0,1:T(8,128)(2,1)} async-done(((bf16[256,5248]{0,1:T(8,128)(2,1)}), bf16[256,5248]{0,1:T(8,128)(2,1)}) %all-reduce.20.cloned.1.call-update) | async-done | bytes 2686992 | tf_op jit(solution)/shard_map/psum | solution.py:383
  (589 shorter events, 624.3 us)
Async XLA Ops:
  7.2 284.4 %all-gather.5.cloned.1.call-start = ((), (), s32[]{:S(2)}) async-start(), calls=%async_computation.24 | async-start | bytes 24182784 | tf_op jit(solution)/shard_map/all_gather | solution.py:184
  11.2 344.2 %all-gather.7.cloned.1.call-start = ((), (), s32[]{:S(2)}) async-start(), calls=%async_computation.25 | async-start | bytes 18874368 | tf_op jit(solution)/shard_map/all_gather | solution.py:184
  21.9 48.4 %collective-permute-start = (bf16[264,2048]{1,0:T(8,128)(2,1)}, bf16[264,2048]{1,0:T(8,128)(2,1)}, u32[]{:S(2)}, u32[]{:S(2)}) collective-permute-start(bf16[264,2048]{1,0:T(8,128)(2,1)} %get-tuple-element.196), channel_id=1, source_target_pairs={{0,8},{8,0},{16,24},{24,16},{1,9},{9,1},{17,25},{25,17},{2,10},{10... | collective-permute-start | bytes 3244040 | tf_op jit(solution)/shard_map/ppermute | solution.py:178
  21.9 92.8 %collective-permute-start.1 = (bf16[264,2048]{1,0:T(8,128)(2,1)}, bf16[264,2048]{1,0:T(8,128)(2,1)}, u32[]{:S(2)}, u32[]{:S(2)}) collective-permute-start(bf16[264,2048]{1,0:T(8,128)(2,1)} %get-tuple-element.195), channel_id=1, source_target_pairs={{0,16},{8,24},{16,0},{24,8},{1,17},{9,25},{17,1},{25,9},{2,18},{10... | collective-permute-start | bytes 3244040 | tf_op jit(solution)/shard_map/ppermute | solution.py:178
  120.9 56.3 %all-to-all-start = ((bf16[8,80,2048]{2,1,0:T(8,128)(2,1)}), bf16[8,80,2048]{2,1,0:T(8,128)(2,1)}, u32[]{:S(2)}, u32[]{:S(2)}) async-start(bf16[8,80,2048]{2,1,0:T(8,128)(2,1)} %bitcast.391), calls=%async_computation | async-start | bytes 5242880 | tf_op jit(solution)/shard_map/all_to_all | solution.py:181
  177.1 64.5 %all-to-all-start.1 = ((bf16[8,80,2048]{2,1,0:T(8,128)(2,1)}), bf16[8,80,2048]{2,1,0:T(8,128)(2,1)}, u32[]{:S(2)}, u32[]{:S(2)}) async-start(bf16[8,80,2048]{2,1,0:T(8,128)(2,1)} %bitcast.390), calls=%async_computation.1 | async-start | bytes 5242880 | tf_op jit(solution)/shard_map/all_to_all | solution.py:181
  241.6 45.3 %all-to-all-start.2 = ((bf16[8,80,2048]{2,1,0:T(8,128)(2,1)}), bf16[8,80,2048]{2,1,0:T(8,128)(2,1)}, u32[]{:S(2)}, u32[]{:S(2)}) async-start(bf16[8,80,2048]{2,1,0:T(8,128)(2,1)} %bitcast.388), calls=%async_computation.2 | async-start | bytes 5242880 | tf_op jit(solution)/shard_map/all_to_all | solution.py:181
  287.0 68.5 %all-to-all-start.3 = ((bf16[8,80,2048]{2,1,0:T(8,128)(2,1)}), bf16[8,80,2048]{2,1,0:T(8,128)(2,1)}, u32[]{:S(2)}, u32[]{:S(2)}) async-start(bf16[8,80,2048]{2,1,0:T(8,128)(2,1)} %bitcast.385), calls=%async_computation.3 | async-start | bytes 5242880 | tf_op jit(solution)/shard_map/all_to_all | solution.py:181
  375.1 43.4 %all-to-all-start.9 = ((bf16[8,80,2048]{2,1,0:T(8,128)(2,1)}), bf16[8,80,2048]{2,1,0:T(8,128)(2,1)}, u32[]{:S(2)}, u32[]{:S(2)}) async-start(bf16[8,80,2048]{2,1,0:T(8,128)(2,1)} %bitcast.384), calls=%async_computation.9 | async-start | bytes 5242880 | tf_op jit(solution)/shard_map/all_to_all | solution.py:181
  388.2 67.9 %collective-permute-start.7 = (bf16[264,2048]{1,0:T(8,128)(2,1)}, bf16[264,2048]{1,0:T(8,128)(2,1)}, u32[]{:S(2)}, u32[]{:S(2)}) collective-permute-start(bf16[264,2048]{1,0:T(8,128)(2,1)} %get-tuple-element.191), channel_id=1, source_target_pairs={{0,8},{8,0},{16,24},{24,16},{1,9},{9,1},{17,25},{25,17},{2,10},{10... | collective-permute-start | bytes 3244040 | tf_op jit(solution)/shard_map/ppermute | solution.py:178
  418.5 79.5 %all-to-all-start.7 = ((bf16[8,80,2048]{2,1,0:T(8,128)(2,1)}), bf16[8,80,2048]{2,1,0:T(8,128)(2,1)}, u32[]{:S(2)}, u32[]{:S(2)}) async-start(bf16[8,80,2048]{2,1,0:T(8,128)(2,1)} %bitcast.386), calls=%async_computation.7 | async-start | bytes 5242880 | tf_op jit(solution)/shard_map/all_to_all | solution.py:181
  422.9 623.1 %all-gather.9.cloned.1.call-start = ((), (), s32[]{:S(2)}) async-start(), calls=%async_computation.26 | async-start | bytes 9437184 | tf_op jit(solution)/shard_map/all_gather | solution.py:184
  422.9 66.1 %collective-permute-start.3 = (bf16[264,2048]{1,0:T(8,128)(2,1)}, bf16[264,2048]{1,0:T(8,128)(2,1)}, u32[]{:S(2)}, u32[]{:S(2)}) collective-permute-start(bf16[264,2048]{1,0:T(8,128)(2,1)} %get-tuple-element.193), channel_id=1, source_target_pairs={{0,16},{8,24},{16,0},{24,8},{1,17},{9,25},{17,1},{25,9},{2,18},{10... | collective-permute-start | bytes 3244040 | tf_op jit(solution)/shard_map/ppermute | solution.py:178
  497.9 41.8 %all-to-all-start.4 = ((bf16[8,80,2048]{2,1,0:T(8,128)(2,1)}), bf16[8,80,2048]{2,1,0:T(8,128)(2,1)}, u32[]{:S(2)}, u32[]{:S(2)}) async-start(bf16[8,80,2048]{2,1,0:T(8,128)(2,1)} %bitcast.389), calls=%async_computation.4 | async-start | bytes 5242880 | tf_op jit(solution)/shard_map/all_to_all | solution.py:181
  772.1 89.6 %collective-permute-start.9 = (bf16[264,2048]{1,0:T(8,128)(2,1)}, bf16[264,2048]{1,0:T(8,128)(2,1)}, u32[]{:S(2)}, u32[]{:S(2)}) collective-permute-start(bf16[264,2048]{1,0:T(8,128)(2,1)} %pad_maximum_fusion.11), channel_id=1, source_target_pairs={{0,16},{8,24},{16,0},{24,8},{1,17},{9,25},{17,1},{25,9},{2,18},{10... | collective-permute-start | bytes 3244040 | tf_op jit(solution)/shard_map/ppermute | solution.py:178
  776.1 86.5 %collective-permute-start.11 = (bf16[264,2048]{1,0:T(8,128)(2,1)}, bf16[264,2048]{1,0:T(8,128)(2,1)}, u32[]{:S(2)}, u32[]{:S(2)}) collective-permute-start(bf16[264,2048]{1,0:T(8,128)(2,1)} %pad_maximum_fusion.13), channel_id=1, source_target_pairs={{0,8},{8,0},{16,24},{24,16},{1,9},{9,1},{17,25},{25,17},{2,10},{10... | collective-permute-start | bytes 3244040 | tf_op jit(solution)/shard_map/ppermute | solution.py:178
  793.1 121.7 %all-to-all-start.13 = ((bf16[8,80,2048]{2,1,0:T(8,128)(2,1)}), bf16[8,80,2048]{2,1,0:T(8,128)(2,1)}, u32[]{:S(2)}, u32[]{:S(2)}) async-start(bf16[8,80,2048]{2,1,0:T(8,128)(2,1)} %bitcast.396), calls=%async_computation.13 | async-start | bytes 5242880 | tf_op jit(solution)/shard_map/all_to_all | solution.py:181
  797.6 272.7 %all-gather.11.cloned.1.call-start = ((), (), s32[]{:S(2)}) async-start(), calls=%async_computation.27 | async-start | bytes 9437184 | tf_op jit(solution)/shard_map/all_gather | solution.py:184
  1015.1 84.0 %collective-permute-start.8 = (bf16[256,2048]{1,0:T(8,128)(2,1)}, bf16[256,2048]{1,0:T(8,128)(2,1)}, u32[]{:S(2)}, u32[]{:S(2)}) collective-permute-start(bf16[256,2048]{1,0:T(8,128)(2,1)} %fusion.101), channel_id=1, source_target_pairs={{0,8},{8,0},{16,24},{24,16},{1,9},{9,1},{17,25},{25,17},{2,10},{10... | collective-permute-start | bytes 3145736 | tf_op jit(solution)/shard_map/ppermute | solution.py:178
  1020.5 78.7 %collective-permute-start.6 = (bf16[256,2048]{1,0:T(8,128)(2,1)}, bf16[256,2048]{1,0:T(8,128)(2,1)}, u32[]{:S(2)}, u32[]{:S(2)}) collective-permute-start(bf16[256,2048]{1,0:T(8,128)(2,1)} %fusion.100), channel_id=1, source_target_pairs={{0,24},{8,16},{16,8},{24,0},{1,25},{9,17},{17,9},{25,1},{2,26},{10... | collective-permute-start | bytes 3145736 | tf_op jit(solution)/shard_map/ppermute | solution.py:178
  1037.8 110.2 %collective-permute-start.5 = (bf16[256,2048]{1,0:T(8,128)(2,1)}, bf16[256,2048]{1,0:T(8,128)(2,1)}, u32[]{:S(2)}, u32[]{:S(2)}) collective-permute-start(bf16[256,2048]{1,0:T(8,128)(2,1)} %fusion.99), channel_id=1, source_target_pairs={{0,16},{8,24},{16,0},{24,8},{1,17},{9,25},{17,1},{25,9},{2,18},{10... | collective-permute-start | bytes 3145736 | tf_op jit(solution)/shard_map/ppermute | solution.py:178
  1070.1 114.7 %all-reduce.18.cloned.1.call-start = ((), (), s32[]{:S(2)}) async-start(), calls=%async_computation.28 | async-start | bytes 4194304 | tf_op jit(solution)/shard_map/psum | solution.py:378
  1080.3 74.4 %all-to-all-start.21 = ((bf16[8,256,640]{2,1,0:T(8,128)(2,1)}), bf16[8,256,640]{2,1,0:T(8,128)(2,1)}, u32[]{:S(2)}, u32[]{:S(2)}) async-start(bf16[8,256,640]{2,1,0:T(8,128)(2,1)} %bitcast.399), calls=%async_computation.21 | async-start | bytes 5242880 | tf_op jit(solution)/shard_map/all_to_all | solution.py:181
  1084.7 209.7 %all-reduce.20.cloned.1.call-start = ((), (), s32[]{:S(2)}) async-start(), calls=%async_computation.29 | async-start | bytes 5373952 | tf_op jit(solution)/shard_map/psum | solution.py:383
  (161 other events, 2651.4 us)
Sparse Core Ops, SparseCore 0:
  11.4 112.3 all-gather.4
  125.7 150.0 all-gather.6
  441.4 76.0 all-gather.8
  873.8 58.0 all-gather.10
  1080.4 104.2 all-reduce.17
  1187.6 106.8 all-reduce.19
